TPU v7x, 32 devices: a whole 2x2x4 slice. The times are simulated.
32 devices in a mesh: rep: 8 (over y, x, core), cp: 4 (over z).
Axes of the slice: x: 2, y: 2, z: 4, core: 2. Of those that a mesh axis runs over, the one named last changes fastest.
Arguments:
- block_input: bfloat16 [4096, 768], P(('rep', 'cp')), may hold values from -6 to 6
- qkv_weight: bfloat16 [768, 2304], P('cp'), may hold values from -4 to 4
- qkv_bias: bfloat16 [2304], P('cp'), may hold values from -3 to 3
- proj_weight: bfloat16 [768, 768], P('cp'), may hold values from -2.5 to 2.5
- proj_bias: bfloat16 [768], P('cp'), may hold values from -3 to 3
- up_weight: bfloat16 [768, 3072], P('cp'), may hold values from -0.21875 to 0.21875
- up_bias: bfloat16 [3072], P('cp'), may hold values from -3 to 3
- down_weight: bfloat16 [3072, 768], P('cp'), may hold values from -0.109375 to 0.109375
- down_bias: bfloat16 [768], P('cp'), may hold values from -3 to 3
- attention_gain: bfloat16 [768], P('cp'), may hold values from 0.099609375 to 1.8984375
- attention_shift: bfloat16 [768], P('cp'), may hold values from -3 to 3
- feed_gain: bfloat16 [768], P('cp'), may hold values from 0.099609375 to 1.8984375
- feed_shift: bfloat16 [768], P('cp'), may hold values from -3 to 3
- out_cotangent: bfloat16 [4096, 768], P(('rep', 'cp')), may hold values from -6 to 6
Outputs:
- block_output: bfloat16 [4096, 768], P(('rep', 'cp'))
- input_grad: float32 [4096, 768], P(('rep', 'cp'))
- qkv_weight_grad: float32 [768, 2304], P('cp')
- qkv_bias_grad: float32 [2304], P('cp')
- proj_weight_grad: float32 [768, 768], P('cp')
- proj_bias_grad: float32 [768], P('cp')
- up_weight_grad: float32 [768, 3072], P('cp')
- up_bias_grad: float32 [3072], P('cp')
- down_weight_grad: float32 [3072, 768], P('cp')
- down_bias_grad: float32 [768], P('cp')
- attention_gain_grad: float32 [768], P('cp')
- attention_shift_grad: float32 [768], P('cp')
- feed_gain_grad: float32 [768], P('cp')
- feed_shift_grad: float32 [768], P('cp')
All inputs are finite; a program needn't handle non-finite values.
Results may differ from a plain program's by a relative error of at most 0.013.
Values may be sent and summed in bfloat16 or wider, within the bound.
A program may use at most 128 MiB of HBM per device.

v0:
```python
import jax
import jax.numpy as jnp
from jax import lax
from jax.sharding import PartitionSpec as P

HEAD = 64
ROT = 16


EPSILON = 1e-05
ROOT_HALF = 0.7071067811865476
INV_ROOT_TWO_PI = 0.3989422804014327


def layer_norm(inputs, norm_gain, norm_shift):
    center = inputs - jnp.mean(inputs, axis=-1, keepdims=True)
    inverse = lax.rsqrt(jnp.mean(center * center, axis=-1, keepdims=True) + EPSILON)
    normed = center * inverse
    return (
        normed * norm_gain.astype(jnp.float32) + norm_shift.astype(jnp.float32),
        normed,
        inverse,
    )


def norm_back(upstream, normed, inverse, norm_gain):
    scaled = upstream * norm_gain.astype(jnp.float32)
    return inverse * (
        scaled
        - jnp.mean(scaled, axis=-1, keepdims=True)
        - normed * jnp.mean(scaled * normed, axis=-1, keepdims=True)
    )


def rotary_tables(positions):
    half_rot = ROT // 2
    inverse_freq = 1.0 / 10000.0 ** (jnp.arange(half_rot, dtype=jnp.float32) * (2.0 / ROT))
    angles = positions.astype(jnp.float32)[:, None] * inverse_freq[None, :]
    cos_table = jnp.concatenate([jnp.cos(angles), jnp.cos(angles)], axis=-1)
    sin_table = jnp.concatenate([jnp.sin(angles), jnp.sin(angles)], axis=-1)
    return (cos_table, sin_table)


def rotate(heads_in, cos_table, sin_table):
    half_rot = ROT // 2
    rotary_part = heads_in[..., :ROT]
    turned = jnp.concatenate([-rotary_part[..., half_rot:], rotary_part[..., :half_rot]], axis=-1)
    rotated = rotary_part * cos_table[:, None, :] + turned * sin_table[:, None, :]
    return jnp.concatenate([rotated, heads_in[..., ROT:]], axis=-1)


def rotate_back(heads_grad, cos_table, sin_table):
    half_rot = ROT // 2
    sined = heads_grad[..., :ROT] * sin_table[:, None, :]
    swapped = jnp.concatenate([sined[..., half_rot:], -sined[..., :half_rot]], axis=-1)
    rotated = heads_grad[..., :ROT] * cos_table[:, None, :] + swapped
    return jnp.concatenate([rotated, heads_grad[..., ROT:]], axis=-1)


def gelu_slope(preact):
    return (
        0.5 * (1.0 + lax.erf(preact * ROOT_HALF))
        + preact * jnp.exp(-0.5 * preact * preact) * INV_ROOT_TWO_PI
    )


def body(
    block_input,
    qkv_weight,
    qkv_bias,
    proj_weight,
    proj_bias,
    up_weight,
    up_bias,
    down_weight,
    down_bias,
    attention_gain,
    attention_shift,
    feed_gain,
    feed_shift,
    out_cotangent,
):
    group_size = lax.axis_size("cp")
    group_rank = lax.axis_index("cp")
    row_count = block_input.shape[0]
    model_width = block_input.shape[1]
    head_count = model_width // HEAD
    total_rows = row_count * group_size
    score_scale = HEAD ** (-0.5)
    gathered = (
        lax.all_gather(qkv_weight, "cp", axis=0, tiled=True),
        lax.all_gather(qkv_bias, "cp", axis=0, tiled=True),
        lax.all_gather(proj_weight, "cp", axis=0, tiled=True),
        lax.all_gather(proj_bias, "cp", axis=0, tiled=True),
        lax.all_gather(up_weight, "cp", axis=0, tiled=True),
        lax.all_gather(up_bias, "cp", axis=0, tiled=True),
        lax.all_gather(down_weight, "cp", axis=0, tiled=True),
        lax.all_gather(down_bias, "cp", axis=0, tiled=True),
        lax.all_gather(attention_gain, "cp", axis=0, tiled=True),
        lax.all_gather(attention_shift, "cp", axis=0, tiled=True),
        lax.all_gather(feed_gain, "cp", axis=0, tiled=True),
        lax.all_gather(feed_shift, "cp", axis=0, tiled=True),
    )
    (
        joined_matrix,
        joined_offset,
        proj_matrix,
        proj_offset,
        up_matrix,
        up_offset,
        down_matrix,
        down_offset,
        gain_one,
        shift_one,
        gain_two,
        shift_two,
    ) = gathered
    positions = group_rank * row_count + jnp.arange(row_count, dtype=jnp.int32)
    key_places = jnp.arange(total_rows, dtype=jnp.int32)
    cos_table, sin_table = rotary_tables(positions)
    widened = block_input.astype(jnp.float32)
    norm_one, normed_one, inverse_one = layer_norm(widened, gain_one, shift_one)
    norm_two, normed_two, inverse_two = layer_norm(widened, gain_two, shift_two)
    attn_in = norm_one.astype(jnp.bfloat16)
    feed_in = norm_two.astype(jnp.bfloat16)
    joined_out = jnp.dot(
        attn_in, joined_matrix, preferred_element_type=jnp.float32
    ) + joined_offset.astype(jnp.float32)
    queries = rotate(
        joined_out[:, :model_width].reshape(row_count, head_count, HEAD), cos_table, sin_table
    ).astype(jnp.bfloat16)
    keys_own = (
        rotate(
            joined_out[:, model_width : 2 * model_width].reshape(row_count, head_count, HEAD),
            cos_table,
            sin_table,
        )
        .astype(jnp.bfloat16)
        .reshape(row_count, model_width)
    )
    values_own = joined_out[:, 2 * model_width :].astype(jnp.bfloat16)
    keys_all, values_all = (
        lax.all_gather(keys_own, "cp", axis=0, tiled=True),
        lax.all_gather(values_own, "cp", axis=0, tiled=True),
    )
    key_heads = keys_all.reshape(total_rows, head_count, HEAD)
    value_heads = values_all.reshape(total_rows, head_count, HEAD)
    causal = positions[:, None] >= key_places[None, :]
    scores = (
        jnp.einsum("thd,shd->hts", queries, key_heads, preferred_element_type=jnp.float32)
        * score_scale
    )
    scores = jnp.where(causal[None], scores, -jnp.inf)
    top_score = jnp.max(scores, axis=-1, keepdims=True)
    log_total = top_score + jnp.log(jnp.sum(jnp.exp(scores - top_score), axis=-1, keepdims=True))
    probs_low = jnp.exp(scores - log_total).astype(jnp.bfloat16)
    context = (
        jnp.einsum("hts,shd->thd", probs_low, value_heads, preferred_element_type=jnp.float32)
        .reshape(row_count, model_width)
        .astype(jnp.bfloat16)
    )
    attention_out = jnp.dot(
        context, proj_matrix, preferred_element_type=jnp.float32
    ) + proj_offset.astype(jnp.float32)
    pre_act = jnp.dot(feed_in, up_matrix, preferred_element_type=jnp.float32) + up_offset.astype(
        jnp.float32
    )
    activated = (0.5 * pre_act * (1.0 + lax.erf(pre_act * ROOT_HALF))).astype(jnp.bfloat16)
    feed_out = jnp.dot(
        activated, down_matrix, preferred_element_type=jnp.float32
    ) + down_offset.astype(jnp.float32)
    block_output = (widened + attention_out + feed_out).astype(jnp.bfloat16)
    back_joined, back_proj, back_up, back_down, back_gain_one, back_gain_two = (
        lax.all_gather(qkv_weight, "cp", axis=0, tiled=True),
        lax.all_gather(proj_weight, "cp", axis=0, tiled=True),
        lax.all_gather(up_weight, "cp", axis=0, tiled=True),
        lax.all_gather(down_weight, "cp", axis=0, tiled=True),
        lax.all_gather(attention_gain, "cp", axis=0, tiled=True),
        lax.all_gather(feed_gain, "cp", axis=0, tiled=True),
    )
    upstream = out_cotangent.astype(jnp.float32)
    bias_sum = jnp.sum(upstream, axis=0)
    down_grad = jnp.dot(activated.T, out_cotangent, preferred_element_type=jnp.float32)
    pre_grad = jnp.dot(out_cotangent, back_down.T, preferred_element_type=jnp.float32) * gelu_slope(
        pre_act
    )
    pre_low = pre_grad.astype(jnp.bfloat16)
    up_grad = jnp.dot(feed_in.T, pre_low, preferred_element_type=jnp.float32)
    up_bgrad = jnp.sum(pre_grad, axis=0)
    feed_in_grad = jnp.dot(pre_low, back_up.T, preferred_element_type=jnp.float32)
    feed_gain_term = jnp.sum(feed_in_grad * normed_two, axis=0)
    feed_shift_term = jnp.sum(feed_in_grad, axis=0)
    proj_grad = jnp.dot(context.T, out_cotangent, preferred_element_type=jnp.float32)
    context_grad = (
        jnp.dot(out_cotangent, back_proj.T, preferred_element_type=jnp.float32)
        .astype(jnp.bfloat16)
        .reshape(row_count, head_count, HEAD)
    )
    row_dots = jnp.sum(
        context_grad.astype(jnp.float32)
        * context.reshape(row_count, head_count, HEAD).astype(jnp.float32),
        axis=-1,
    ).T
    last_position = positions[row_count - 1]
    starting = (
        jnp.zeros((row_count, head_count, HEAD), jnp.float32),
        jnp.zeros((total_rows, model_width), jnp.float32),
        jnp.zeros((total_rows, model_width), jnp.float32),
    )
    piece_keys = lax.all_gather(keys_own, "cp", axis=0, tiled=True)
    piece_values = lax.all_gather(values_own, "cp", axis=0, tiled=True)
    piece_rows = piece_keys.shape[0]

    def accumulate(totals):
        places = jnp.arange(piece_rows, dtype=jnp.int32)
        visible = positions[:, None] >= places[None, :]
        key_part = piece_keys.reshape(piece_rows, head_count, HEAD)
        value_part = piece_values.reshape(piece_rows, head_count, HEAD)
        part_scores = (
            jnp.einsum("thd,shd->hts", queries, key_part, preferred_element_type=jnp.float32)
            * score_scale
        )
        part_scores = jnp.where(visible[None], part_scores, -jnp.inf)
        part_probs = jnp.exp(part_scores - log_total)
        probs_grad = jnp.einsum(
            "thd,shd->hts", context_grad, value_part, preferred_element_type=jnp.float32
        )
        score_grad = (part_probs * (probs_grad - row_dots[:, :, None]) * score_scale).astype(
            jnp.bfloat16
        )
        query_acc = jnp.einsum(
            "hts,shd->thd", score_grad, key_part, preferred_element_type=jnp.float32
        )
        key_term = jnp.einsum(
            "hts,thd->shd", score_grad, queries, preferred_element_type=jnp.float32
        ).reshape(piece_rows, model_width)
        value_term = jnp.einsum(
            "hts,thd->shd",
            part_probs.astype(jnp.bfloat16),
            context_grad,
            preferred_element_type=jnp.float32,
        ).reshape(piece_rows, model_width)
        return (query_acc, key_term, value_term)

    def unchanged(totals):
        return totals

    query_grad, key_grad_all, value_grad_all = lax.cond(
        jnp.int32(0) <= last_position, accumulate, unchanged, starting
    )
    key_grad_own, value_grad_own = (
        lax.psum_scatter(key_grad_all, "cp", scatter_dimension=0, tiled=True),
        lax.psum_scatter(value_grad_all, "cp", scatter_dimension=0, tiled=True),
    )
    joined_grad = jnp.concatenate(
        [
            rotate_back(query_grad, cos_table, sin_table).reshape(row_count, model_width),
            rotate_back(
                key_grad_own.reshape(row_count, head_count, HEAD), cos_table, sin_table
            ).reshape(row_count, model_width),
            value_grad_own,
        ],
        axis=1,
    )
    joined_low = joined_grad.astype(jnp.bfloat16)
    qkv_grad = jnp.dot(attn_in.T, joined_low, preferred_element_type=jnp.float32)
    qkv_bgrad = jnp.sum(joined_grad, axis=0)
    attn_in_grad = jnp.dot(joined_low, back_joined.T, preferred_element_type=jnp.float32)
    attn_gain_term = jnp.sum(attn_in_grad * normed_one, axis=0)
    attn_shift_term = jnp.sum(attn_in_grad, axis=0)
    input_grad = (
        upstream
        + norm_back(attn_in_grad, normed_one, inverse_one, back_gain_one)
        + norm_back(feed_in_grad, normed_two, inverse_two, back_gain_two)
    )
    (
        owned_qkv,
        owned_qkvb,
        owned_proj,
        owned_projb,
        owned_up,
        owned_upb,
        owned_down,
        owned_downb,
        owned_gainone,
        owned_shiftone,
        owned_gaintwo,
        owned_shifttwo,
    ) = (
        lax.psum_scatter(qkv_grad, "cp", scatter_dimension=0, tiled=True),
        lax.psum_scatter(qkv_bgrad, "cp", scatter_dimension=0, tiled=True),
        lax.psum_scatter(proj_grad, "cp", scatter_dimension=0, tiled=True),
        lax.psum_scatter(bias_sum, "cp", scatter_dimension=0, tiled=True),
        lax.psum_scatter(up_grad, "cp", scatter_dimension=0, tiled=True),
        lax.psum_scatter(up_bgrad, "cp", scatter_dimension=0, tiled=True),
        lax.psum_scatter(down_grad, "cp", scatter_dimension=0, tiled=True),
        lax.psum_scatter(bias_sum, "cp", scatter_dimension=0, tiled=True),
        lax.psum_scatter(attn_gain_term, "cp", scatter_dimension=0, tiled=True),
        lax.psum_scatter(attn_shift_term, "cp", scatter_dimension=0, tiled=True),
        lax.psum_scatter(feed_gain_term, "cp", scatter_dimension=0, tiled=True),
        lax.psum_scatter(feed_shift_term, "cp", scatter_dimension=0, tiled=True),
    )
    (
        summed_qkv,
        summed_qkvb,
        summed_proj,
        summed_projb,
        summed_up,
        summed_upb,
        summed_down,
        summed_downb,
        summed_gainone,
        summed_shiftone,
        summed_gaintwo,
        summed_shifttwo,
    ) = lax.psum(
        (
            owned_qkv,
            owned_qkvb,
            owned_proj,
            owned_projb,
            owned_up,
            owned_upb,
            owned_down,
            owned_downb,
            owned_gainone,
            owned_shiftone,
            owned_gaintwo,
            owned_shifttwo,
        ),
        "rep",
    )
    return (
        block_output,
        input_grad,
        summed_qkv,
        summed_qkvb,
        summed_proj,
        summed_projb,
        summed_up,
        summed_upb,
        summed_down,
        summed_downb,
        summed_gainone,
        summed_shiftone,
        summed_gaintwo,
        summed_shifttwo,
    )


def solution(mesh):
    return jax.shard_map(
        body,
        mesh=mesh,
        in_specs=(
            P(("rep", "cp"), None),
            P("cp", None),
            P("cp"),
            P("cp", None),
            P("cp"),
            P("cp", None),
            P("cp"),
            P("cp", None),
            P("cp"),
            P("cp"),
            P("cp"),
            P("cp"),
            P("cp"),
            P(("rep", "cp"), None),
        ),
        out_specs=(
            P(("rep", "cp"), None),
            P(("rep", "cp"), None),
            P("cp", None),
            P("cp"),
            P("cp", None),
            P("cp"),
            P("cp", None),
            P("cp"),
            P("cp", None),
            P("cp"),
            P("cp"),
            P("cp"),
            P("cp"),
            P("cp"),
        ),
        check_vma=False,
    )
```

profile of v0, /device:TPU:11, one launch (start us, length us, event | category | flops | bytes accessed | tf_op | source)
XLA Modules:
  0.0 1048.1 jit_solution(9973064314887172787)
XLA Ops:
  7.2 0.7 all-gather.8.cloned.1.call-update
  8.0 0.7 all-gather.6.cloned.1.call-update
  8.7 1.3 fusion.73
  11.4 0.6 slice.92
  12.6 0.8 dynamic-update-slice
  13.5 0.8 dynamic-update-slice.1
  14.3 0.8 dynamic-update-slice.4
  15.2 0.8 dynamic-update-slice.5
  16.0 0.8 dynamic-update-slice.6
  16.8 0.8 dynamic-update-slice.3
  17.7 0.9 dynamic-update-slice.2
  18.5 14.4 %all-reduce.17 = (bf16[768]{0:T(1024)(128)(2,1)}, bf16[768]{0:T(1024)(128)(2,1)}, bf16[768]{0:T(1024)(128)(2,1)}, bf16[2304]{0:T(1024)(128)(2,1)S(1)}, bf16[768]...) all-reduce(bf16[768]{0:T(1024)(128)(2,1)S(1)} %dynamic-update-slice, ...), channel_id=1, replica_groups=mesh['rep'=8,'cp'=4] {'cp'}, use_global_device_ids=true, to_apply=%add.6 | all-reduce | flops 6912 | bytes 27648
  33.1 1.0 convert_reduce_fusion
  34.5 6.9 all-gather.8.cloned.1.call-done
  41.5 1.8 convolution_convert_fusion
  43.5 66.9 %all-gather.6.cloned.1.call-done = bf16[768,2304]{1,0:T(8,128)(2,1)} async-done(((bf16[192,2304]{1,0:T(8,128)(2,1)}), bf16[768,2304]{1,0:T(8,128)(2,1)}) %all-gather.6.cloned.1.call-update) | async-done | bytes 3538960 | tf_op jit(solution)/shard_map/all_gather | solution.py:91
  110.3 2.7 convolution_add_fusion
  113.6 17.2 %all_gather.55 = bf16[512,768]{0,1:T(8,128)(2,1)S(1)} all-gather(bf16[128,768]{0,1:T(8,128)(2,1)S(1)} %bitcast.76), channel_id=1, replica_groups=mesh['rep'=8,'cp'=4] {'cp'}, dimensions={0}, use_global_device_ids=true | all-gather | bytes 983040 | tf_op jit(solution)/shard_map/all_gather | solution.py:143
  130.8 15.4 %all_gather.54 = bf16[512,768]{1,0:T(8,128)(2,1)S(1)} all-gather(bf16[128,768]{1,0:T(8,128)(2,1)S(1)} %slice.137), channel_id=1, replica_groups=mesh['rep'=8,'cp'=4] {'cp'}, dimensions={0}, use_global_device_ids=true | all-gather | bytes 983040 | tf_op jit(solution)/shard_map/all_gather | solution.py:144
  146.2 1.2 copy.45
  147.4 0.7 fusion.9
  148.1 0.9 exponential_reduce_fusion
  149.3 2.3 multiply_reduce_fusion
  151.5 5.6 conditional.1
  152.0 0.6 fusion.75
  152.6 1.4 multiply_convert_fusion
  154.0 1.0 fusion.1
  155.0 0.6 convolution_bitcast_fusion
  155.6 1.5 fusion.76
  157.3 1.1 copy-done.1
  158.4 0.5 all-gather.10.cloned.1.call-update
  159.6 1.9 fusion.77
  161.5 33.4 %reduce-scatter.7.cloned.1.call-done = f32[128,768]{0,1:T(8,128)} async-done(((f32[512,768]{0,1:T(8,128)}), f32[128,768]{0,1:T(8,128)}) %reduce-scatter.7.cloned.1.call-update) | async-done | bytes 393232 | tf_op jit(solution)/shard_map/reduce_scatter | solution.py:252
  195.0 1.0 slice.117
  196.0 0.9 broadcast_multiply_fusion
  196.9 0.9 maximum_add_fusion
  197.9 34.1 %reduce-scatter.9.cloned.1.call-done = f32[128,768]{0,1:T(8,128)} async-done(((f32[512,768]{0,1:T(8,128)}), f32[128,768]{0,1:T(8,128)}) %reduce-scatter.9.cloned.1.call-update) | async-done | bytes 393232 | tf_op jit(solution)/shard_map/reduce_scatter | solution.py:253
  232.0 5.1 fusion.60
  237.9 12.0 %all-gather = bf16[4,1,768]{2,1,0:T(2,128)(2,1)S(1)} all-gather(bf16[1,1,768]{2,1,0:T(2,128)(2,1)S(1)} %reshape.211), channel_id=1, replica_groups=mesh['rep'=8,'cp'=4] {'cp'}, dimensions={0}, use_global_device_ids=true | all-gather | bytes 7680 | tf_op jit(solution)/shard_map/all_gather | solution.py:96
  249.9 71.3 %all-gather.10.cloned.1.call-done = bf16[768,3072]{1,0:T(8,128)(2,1)} async-done(((bf16[192,3072]{1,0:T(8,128)(2,1)}), bf16[768,3072]{1,0:T(8,128)(2,1)}) %all-gather.10.cloned.1.call-update) | async-done | bytes 4718608 | tf_op jit(solution)/shard_map/all_gather | solution.py:95
  321.2 3.2 convolution_add_fusion.1
  324.4 5.1 fusion.69
  329.5 81.0 %all-gather.12.cloned.1.call-done = bf16[3072,768]{1,0:T(8,128)(2,1)} async-done(((bf16[768,768]{1,0:T(8,128)(2,1)}), bf16[3072,768]{1,0:T(8,128)(2,1)}) %all-gather.12.cloned.1.call-update) | async-done | bytes 4718608 | tf_op jit(solution)/shard_map/all_gather | solution.py:97
  410.5 4.7 fusion.74
  415.1 5.8 fusion.49
  421.0 40.4 %reduce-scatter.13.cloned.1.call-done = f32[192,768]{1,0:T(8,128)} async-done(((f32[768,768]{1,0:T(8,128)}), f32[192,768]{1,0:T(8,128)}) %reduce-scatter.13.cloned.1.call-update) | async-done | bytes 589840 | tf_op jit(solution)/shard_map/reduce_scatter | solution.py:292
  461.4 125.9 %reduce-scatter.11.cloned.1.call-done = f32[192,2304]{1,0:T(8,128)} async-done(((f32[768,2304]{1,0:T(8,128)}), f32[192,2304]{1,0:T(8,128)}) %reduce-scatter.11.cloned.1.call-update) | async-done | bytes 1769488 | tf_op jit(solution)/shard_map/reduce_scatter | solution.py:290
  587.4 164.0 %reduce-scatter.17.cloned.1.call-done = f32[768,768]{1,0:T(8,128)} async-done(((f32[3072,768]{1,0:T(8,128)}), f32[768,768]{1,0:T(8,128)}) %reduce-scatter.17.cloned.1.call-update) | async-done | bytes 2359312 | tf_op jit(solution)/shard_map/reduce_scatter | solution.py:296
  751.4 164.4 %reduce-scatter.15.cloned.1.call-done = f32[192,3072]{1,0:T(8,128)} async-done(((f32[768,3072]{1,0:T(8,128)}), f32[192,3072]{1,0:T(8,128)}) %reduce-scatter.15.cloned.1.call-update) | async-done | bytes 2359312 | tf_op jit(solution)/shard_map/reduce_scatter | solution.py:294
  917.8 0.7 convert_element_type.113
  918.4 3.3 convolution_add_fusion.3
  921.8 1.1 fusion.22
  922.9 4.2 fusion.51
  927.4 1.5 fusion.46
  929.0 1.0 convert_reduce_fusion.1
  930.1 13.2 %all-reduce.16 = (f32[2304]{0:T(1024)S(1)}, f32[768]{0:T(1024)S(1)}, f32[3072]{0:T(1024)S(1)}, f32[768]{0:T(1024)S(1)}, f32[768]{0:T(1024)S(1)}, /*index=5*/f32[768]{0:T(1024)S(1)}, f32[768]{0:T(1024)S(1)}) all-reduce(f32[2304]{0:T(1024)S(1)} %fusion.23, ...), channel_id=5, replica_groups=mesh['rep'=8,'cp'=4] {'cp'}, use_global_device_ids=true, to_apply=%region_16.17.clone | all-reduce | flops 9216 | bytes 73728
  943.8 24.9 %all-reduce.14 = (f32[576]{0:T(1024)}, f32[192]{0:T(256)S(1)}, f32[768]{0:T(1024)}, f32[192]{0:T(256)}, f32[192]{0:T(256)}, /*index=5*/f32[192]{0:T(256)}, f32[192]{0:T(256)}) all-reduce(f32[576]{0:T(1024)S(1)} %dynamic-slice.8, f32[192]{0:T(256)S(1)} %dynamic-slice.10, ...), channel_id=1, replica_groups=mesh['rep'=8,'cp'=4] {'rep'}, use_global_device_ids=true, to_apply=%region_17.18 | all-reduce | flops 2304 | bytes 18432 | tf_op jit(solution)/shard_map/psum | solution.py:316
  968.8 64.5 %all-reduce.20.cloned.1.call-done = (f32[192,2304]{1,0:T(8,128)}, f32[192,768]{1,0:T(8,128)}, f32[192,3072]{1,0:T(8,128)}, f32[768,768]{1,0:T(8,128)}) async-done(((f32[192,2304]{1,0:T(8,128)}, f32[192,768]{1,0:T(8,128)}, f32[192,3072]{1,0:T(8,128)}, f32[768,768]{1,0:T(8,128)}), (f32[192,2304]{1,0:T(8,128)}, f32[192,768]{1,0:T(8,128)}, f32[192,3072]{1,0:T(8,128)}, ...) | async-done | bytes 7077904 | tf_op jit(solution)/shard_map/psum | solution.py:316
  1033.3 0.6 copy.70
  1033.8 2.9 copy.71
  1036.8 0.8 copy.72
  1037.6 1.4 copy.73
  1039.0 1.1 copy-done.5
  1040.1 1.4 copy.74
  (136 shorter events, 4.7 us)
Async XLA Ops:
  7.2 27.0 %copy-start = (bf16[128,768]{1,0:T(8,128)(2,1)S(1)}, bf16[128,768]{1,0:T(8,128)(2,1)}, u32[]{:S(2)}) copy-start(bf16[128,768]{1,0:T(8,128)(2,1)} %param.16) | copy-start | bytes 589828
  7.2 34.3 %copy-start.4 = (bf16[128,768]{1,0:T(8,128)(2,1)S(1)}, bf16[128,768]{1,0:T(8,128)(2,1)}, u32[]{:S(2)}) copy-start(bf16[128,768]{1,0:T(8,128)(2,1)} %param.29) | copy-start | bytes 589828
  7.2 34.3 %all-gather.8.cloned.1.call-start = ((), (), s32[]{:S(2)}) async-start(), calls=%async_computation.7 | async-start | bytes 1474560 | tf_op jit(solution)/shard_map/all_gather | solution.py:93
  7.9 102.4 %all-gather.6.cloned.1.call-start = ((), (), s32[]{:S(2)}) async-start(), calls=%async_computation.6 | async-start | bytes 4423680 | tf_op jit(solution)/shard_map/all_gather | solution.py:91
  8.7 186.3 %reduce-scatter.7.cloned.1.call-start = ((), (), s32[]{:S(2)}) async-start(), calls=%async_computation.10 | async-start | bytes 1966080 | tf_op jit(solution)/shard_map/reduce_scatter | solution.py:252
  11.4 30.1 %copy-start.23 = (s32[128]{0:T(128)}, s32[128]{0:T(128)S(1)}, u32[]{:S(2)}) copy-start(s32[128]{0:T(128)S(1)} %iota_add_fusion) | copy-start | bytes 1540
  33.1 80.4 %copy-start.12 = (f32[128,16]{0,1:T(8,128)}, f32[128,16]{0,1:T(8,128)S(1)}, u32[]{:S(2)}) copy-start(f32[128,16]{0,1:T(8,128)S(1)} %get-tuple-element.157) | copy-start | bytes 24580
  33.1 80.4 %copy-start.14 = (f32[128,16]{0,1:T(8,128)}, f32[128,16]{0,1:T(8,128)S(1)}, u32[]{:S(2)}) copy-start(f32[128,16]{0,1:T(8,128)S(1)} %get-tuple-element.158) | copy-start | bytes 24580
  34.2 78.8 %copy-start.16 = (f32[128]{0:T(128)}, f32[128]{0:T(128)S(1)}, u32[]{:S(2)}) copy-start(f32[128]{0:T(128)S(1)} %broadcast_multiply_fusion.5) | copy-start | bytes 1540
  34.4 78.6 %copy-start.18 = (f32[128]{0:T(128)}, f32[128]{0:T(128)S(1)}, u32[]{:S(2)}) copy-start(f32[128]{0:T(128)S(1)} %add_rsqrt_fusion) | copy-start | bytes 1540
  148.1 1.1 copy-start.8
  149.3 2.3 copy-start.24
  151.9 0.7 copy-start.30
  157.2 1.1 copy-start.1
  157.2 74.8 %reduce-scatter.9.cloned.1.call-start = ((), (), s32[]{:S(2)}) async-start(), calls=%async_computation.11 | async-start | bytes 1966080 | tf_op jit(solution)/shard_map/reduce_scatter | solution.py:253
  158.3 1.2 copy-start.9
  158.4 162.8 %all-gather.10.cloned.1.call-start = ((), (), s32[]{:S(2)}) async-start(), calls=%async_computation.8 | async-start | bytes 5898240 | tf_op jit(solution)/shard_map/all_gather | solution.py:95
  158.9 251.5 %all-gather.12.cloned.1.call-start = ((), (), s32[]{:S(2)}) async-start(), calls=%async_computation.9 | async-start | bytes 5898240 | tf_op jit(solution)/shard_map/all_gather | solution.py:97
  159.5 301.9 %reduce-scatter.13.cloned.1.call-start = ((), (), s32[]{:S(2)}) async-start(), calls=%async_computation.13 | async-start | bytes 2949120 | tf_op jit(solution)/shard_map/reduce_scatter | solution.py:292
  161.4 34.5 %copy-start.15 = (f32[128,16]{0,1:T(8,128)S(1)}, f32[128,16]{0,1:T(8,128)}, u32[]{:S(2)}) copy-start(f32[128,16]{0,1:T(8,128)} %copy-done.14) | copy-start | bytes 24580
  161.4 35.5 %copy-start.13 = (f32[128,16]{0,1:T(8,128)S(1)}, f32[128,16]{0,1:T(8,128)}, u32[]{:S(2)}) copy-start(f32[128,16]{0,1:T(8,128)} %copy-done.12) | copy-start | bytes 24580
  161.5 425.9 %reduce-scatter.11.cloned.1.call-start = ((), (), s32[]{:S(2)}) async-start(), calls=%async_computation.12 | async-start | bytes 8847360 | tf_op jit(solution)/shard_map/reduce_scatter | solution.py:290
  195.9 36.1 %copy-start.17 = (f32[128]{0:T(128)S(1)}, f32[128]{0:T(128)}, u32[]{:S(2)}) copy-start(f32[128]{0:T(128)} %copy-done.16) | copy-start | bytes 1540
  196.0 36.1 %copy-start.19 = (f32[128]{0:T(128)S(1)}, f32[128]{0:T(128)}, u32[]{:S(2)}) copy-start(f32[128]{0:T(128)} %copy-done.18) | copy-start | bytes 1540
  237.2 0.7 copy-start.28
  237.2 0.7 copy-start.27
  237.2 0.7 copy-start.26
  237.2 84.0 %copy-start.20 = (f32[128]{0:T(128)S(1)}, f32[128]{0:T(128)}, u32[]{:S(2)}) copy-start(f32[128]{0:T(128)} %copy-done.18) | copy-start | bytes 1540
  237.2 514.2 %reduce-scatter.17.cloned.1.call-start = ((), (), s32[]{:S(2)}) async-start(), calls=%async_computation.15 | async-start | bytes 11796480 | tf_op jit(solution)/shard_map/reduce_scatter | solution.py:296
  329.5 586.3 %reduce-scatter.15.cloned.1.call-start = ((), (), s32[]{:S(2)}) async-start(), calls=%async_computation.14 | async-start | bytes 11796480 | tf_op jit(solution)/shard_map/reduce_scatter | solution.py:294
  421.0 612.3 %all-reduce.20.cloned.1.call-start = ((), (), s32[]{:S(2)}) async-start(), calls=%async_computation.16 | async-start | bytes 14155776 | tf_op jit(solution)/shard_map/psum | solution.py:316
  915.8 2.0 copy-start.25
  918.4 3.4 copy-start.2
  918.4 3.4 copy-start.10
  922.9 4.2 copy-start.7
  922.9 4.6 copy-start.3
  922.9 4.6 copy-start.21
  929.0 1.1 copy-start.22
  968.8 68.0 %copy-start.29 = (f32[192]{0:T(256)}, f32[192]{0:T(256)S(1)}, u32[]{:S(2)}) copy-start(f32[192]{0:T(256)S(1)} %get-tuple-element.204) | copy-start | bytes 2308
  1033.8 3.0 copy-start.11
  1033.8 3.8 copy-start.6
  1037.6 2.5 copy-start.5
Sparse Core Ops, SparseCore 0:
  9.6 31.8 all-gather.7
  43.0 67.2 all-gather.5
  157.3 37.5 reduce-scatter.6
  197.7 34.2 reduce-scatter.8
  233.4 87.7 all-gather.9
  322.6 87.8 all-gather.11
  413.3 48.0 reduce-scatter.12
  463.7 123.5 reduce-scatter.10
  589.7 161.6 reduce-scatter.16
  753.6 162.1 reduce-scatter.14
  919.5 113.7 all-reduce.19
where the time goes:
time: 1050 us
  waiting for transfers between devices  855 us (81%)
  blocking collectives  97.1 us (9%)
  matrix products  48.5 us (5%)
  local copies, waits for them, and re-layouts  21.5 us (2%)
  between operations  18.3 us (2%)
    reduce_scatter x1, waiting for transfers between devices, body(): lax.psum_scatter(up_grad, 'cp', scatter_dimension=0, tiled=True)  164 us
    reduce_scatter x1, waiting for transfers between devices, body(): lax.psum_scatter(down_grad, 'cp', scatter_dimension=0, tiled=True)  164 us
    reduce_scatter x1, waiting for transfers between devices, body(): lax.psum_scatter(qkv_grad, 'cp', scatter_dimension=0, tiled=True)  126 us
    all_gather x1, waiting for transfers between devices, body(): lax.all_gather(down_weight, 'cp', axis=0, tiled=True)  81 us
    all_gather x1, waiting for transfers between devices, body(): lax.all_gather(up_weight, 'cp', axis=0, tiled=True)  71.3 us
    all_gather x1, waiting for transfers between devices, body(): lax.all_gather(qkv_weight, 'cp', axis=0, tiled=True)  66.9 us
    psum x1, waiting for transfers between devices, body(): lax.psum((owned_qkv, owned_qkvb, owned_proj, owned_projb, owned_up, owned...  64.5 us
    reduce_scatter x1, waiting for transfers between devices, body(): lax.psum_scatter(proj_grad, 'cp', scatter_dimension=0, tiled=True)  40.4 us
  transfers between devices with their start and end apart: 11, of which 11 were waited for; matrix products, arithmetic and copies ran while one was open for 5% of the time, Pallas kernels for 0%

commit v1 on v0

v1 whole, which is shorter than its diff:
```python
import jax
import jax.numpy as jnp
from jax import lax
from jax.sharding import PartitionSpec as P

HEAD = 64
ROT = 16


EPSILON = 1e-05
ROOT_HALF = 0.7071067811865476
INV_ROOT_TWO_PI = 0.3989422804014327


def layer_norm(inputs, norm_gain, norm_shift):
    center = inputs - jnp.mean(inputs, axis=-1, keepdims=True)
    inverse = lax.rsqrt(jnp.mean(center * center, axis=-1, keepdims=True) + EPSILON)
    normed = center * inverse
    return (
        normed * norm_gain.astype(jnp.float32) + norm_shift.astype(jnp.float32),
        normed,
        inverse,
    )


def norm_back(upstream, normed, inverse, norm_gain):
    scaled = upstream * norm_gain.astype(jnp.float32)
    return inverse * (
        scaled
        - jnp.mean(scaled, axis=-1, keepdims=True)
        - normed * jnp.mean(scaled * normed, axis=-1, keepdims=True)
    )


def rotary_tables(positions):
    half_rot = ROT // 2
    inverse_freq = 1.0 / 10000.0 ** (jnp.arange(half_rot, dtype=jnp.float32) * (2.0 / ROT))
    angles = positions.astype(jnp.float32)[:, None] * inverse_freq[None, :]
    cos_table = jnp.concatenate([jnp.cos(angles), jnp.cos(angles)], axis=-1)
    sin_table = jnp.concatenate([jnp.sin(angles), jnp.sin(angles)], axis=-1)
    return (cos_table, sin_table)


def rotate(heads_in, cos_table, sin_table):
    half_rot = ROT // 2
    rotary_part = heads_in[..., :ROT]
    turned = jnp.concatenate([-rotary_part[..., half_rot:], rotary_part[..., :half_rot]], axis=-1)
    rotated = rotary_part * cos_table[:, None, :] + turned * sin_table[:, None, :]
    return jnp.concatenate([rotated, heads_in[..., ROT:]], axis=-1)


def rotate_back(heads_grad, cos_table, sin_table):
    half_rot = ROT // 2
    sined = heads_grad[..., :ROT] * sin_table[:, None, :]
    swapped = jnp.concatenate([sined[..., half_rot:], -sined[..., :half_rot]], axis=-1)
    rotated = heads_grad[..., :ROT] * cos_table[:, None, :] + swapped
    return jnp.concatenate([rotated, heads_grad[..., ROT:]], axis=-1)


def gelu_slope(preact):
    return (
        0.5 * (1.0 + lax.erf(preact * ROOT_HALF))
        + preact * jnp.exp(-0.5 * preact * preact) * INV_ROOT_TWO_PI
    )


def body(
    block_input,
    qkv_weight,
    qkv_bias,
    proj_weight,
    proj_bias,
    up_weight,
    up_bias,
    down_weight,
    down_bias,
    attention_gain,
    attention_shift,
    feed_gain,
    feed_shift,
    out_cotangent,
):
    f32, bf16 = jnp.float32, jnp.bfloat16
    group = lax.axis_size("cp")
    reps = lax.axis_size("rep")
    rank = lax.axis_index("cp")
    rows, width = block_input.shape
    own = width // group
    heads = own // HEAD
    total_rows = rows * group
    hidden = up_weight.shape[1] // group
    qkv_cols = 3 * own
    part_cols = qkv_cols + hidden
    score_scale = HEAD ** (-0.5)

    small = jnp.concatenate(
        [qkv_bias, proj_bias, down_bias, attention_gain, attention_shift, feed_gain, feed_shift]
    )
    small_rows = -(-small.shape[0] // width)
    small_block = jnp.pad(small, (0, small_rows * width - small.shape[0])).reshape(
        small_rows, width
    )
    packed = lax.all_gather(
        jnp.concatenate([block_input, out_cotangent, small_block], axis=0), "cp", axis=0
    )
    tokens = packed[:, :rows].reshape(total_rows, width)
    cotangent = packed[:, rows : 2 * rows].reshape(total_rows, width)
    small_all = packed[:, 2 * rows :].reshape(group, small_rows * width)
    joined_offset_all = small_all[:, :qkv_cols].reshape(group * qkv_cols)
    joined_offset = lax.dynamic_slice_in_dim(
        joined_offset_all.reshape(3, group, own), rank, 1, axis=1
    ).reshape(qkv_cols)
    proj_offset, down_offset, gain_one, shift_one, gain_two, shift_two = (
        small_all[:, qkv_cols + i * own : qkv_cols + (i + 1) * own].reshape(width)
        for i in range(6)
    )

    stripes = jnp.concatenate(
        [
            qkv_weight.reshape(own, 3, group, own).transpose(0, 2, 1, 3).reshape(own, group, -1),
            up_weight.reshape(own, group, hidden),
        ],
        axis=2,
    ).reshape(reps, own // reps, group, part_cols)
    mine = lax.dynamic_index_in_dim(stripes, lax.axis_index("rep"), 0, keepdims=False)
    mine = lax.all_to_all(mine.transpose(1, 0, 2), "cp", 0, 0)
    weights = lax.all_gather(mine, "rep", axis=0)
    weights = weights.transpose(1, 0, 2, 3).reshape(width, part_cols)
    joined_matrix = weights[:, :qkv_cols]
    up_matrix = weights[:, qkv_cols:]

    positions = jnp.arange(total_rows, dtype=jnp.int32)
    cos_table, sin_table = rotary_tables(positions)
    widened = tokens.astype(f32)
    center = widened - jnp.mean(widened, axis=-1, keepdims=True)
    inverse = lax.rsqrt(jnp.mean(center * center, axis=-1, keepdims=True) + EPSILON)
    normed = center * inverse
    attn_in = (normed * gain_one.astype(f32) + shift_one.astype(f32)).astype(bf16)
    feed_in = (normed * gain_two.astype(f32) + shift_two.astype(f32)).astype(bf16)

    joined_out = jnp.dot(attn_in, joined_matrix, preferred_element_type=f32) + joined_offset.astype(
        f32
    )
    queries = rotate(
        joined_out[:, :own].reshape(total_rows, heads, HEAD), cos_table, sin_table
    ).astype(bf16)
    keys = rotate(
        joined_out[:, own : 2 * own].reshape(total_rows, heads, HEAD), cos_table, sin_table
    ).astype(bf16)
    values = joined_out[:, 2 * own :].astype(bf16).reshape(total_rows, heads, HEAD)
    causal = positions[:, None] >= positions[None, :]
    scores = jnp.einsum("thd,shd->hts", queries, keys, preferred_element_type=f32) * score_scale
    scores = jnp.where(causal[None], scores, -jnp.inf)
    top_score = jnp.max(scores, axis=-1, keepdims=True)
    log_total = top_score + jnp.log(jnp.sum(jnp.exp(scores - top_score), axis=-1, keepdims=True))
    exact_probs = jnp.exp(scores - log_total)
    probs_low = exact_probs.astype(bf16)
    context = (
        jnp.einsum("hts,shd->thd", probs_low, values, preferred_element_type=f32)
        .reshape(total_rows, own)
        .astype(bf16)
    )
    pre_act = jnp.dot(feed_in, up_matrix, preferred_element_type=f32) + up_bias.astype(f32)
    activated = (0.5 * pre_act * (1.0 + lax.erf(pre_act * ROOT_HALF))).astype(bf16)
    branch_part = jnp.dot(context, proj_weight, preferred_element_type=f32) + jnp.dot(
        activated, down_weight, preferred_element_type=f32
    )

    bias_sum = jnp.sum(out_cotangent.astype(f32), axis=0)
    down_grad = jnp.dot(activated.T, cotangent, preferred_element_type=f32)
    pre_grad = jnp.dot(cotangent, down_weight.T, preferred_element_type=f32) * gelu_slope(pre_act)
    pre_low = pre_grad.astype(bf16)
    up_grad = jnp.dot(feed_in.T, pre_low, preferred_element_type=f32)
    up_bgrad = jnp.sum(pre_grad, axis=0)
    feed_in_grad = jnp.dot(pre_low, up_matrix.T, preferred_element_type=f32)
    proj_grad = jnp.dot(context.T, cotangent, preferred_element_type=f32)
    context_grad = (
        jnp.dot(cotangent, proj_weight.T, preferred_element_type=f32)
        .astype(bf16)
        .reshape(total_rows, heads, HEAD)
    )
    row_dots = jnp.sum(
        context_grad.astype(f32) * context.reshape(total_rows, heads, HEAD).astype(f32), axis=-1
    ).T
    probs_grad = jnp.einsum("thd,shd->hts", context_grad, values, preferred_element_type=f32)
    score_grad = (exact_probs * (probs_grad - row_dots[:, :, None]) * score_scale).astype(bf16)
    query_grad = jnp.einsum("hts,shd->thd", score_grad, keys, preferred_element_type=f32)
    key_grad = jnp.einsum("hts,thd->shd", score_grad, queries, preferred_element_type=f32)
    value_grad = jnp.einsum("hts,thd->shd", probs_low, context_grad, preferred_element_type=f32)
    joined_grad = jnp.concatenate(
        [
            rotate_back(query_grad, cos_table, sin_table).reshape(total_rows, own),
            rotate_back(key_grad, cos_table, sin_table).reshape(total_rows, own),
            value_grad.reshape(total_rows, own),
        ],
        axis=1,
    )
    joined_low = joined_grad.astype(bf16)
    qkv_grad = jnp.dot(attn_in.T, joined_low, preferred_element_type=f32)
    qkv_bgrad = jnp.sum(joined_grad, axis=0)
    attn_in_grad = jnp.dot(joined_low, joined_matrix.T, preferred_element_type=f32)

    scaled_part = attn_in_grad * gain_one.astype(f32) + feed_in_grad * gain_two.astype(f32)
    sums = lax.psum_scatter(
        jnp.concatenate(
            [
                branch_part.reshape(group, rows, width),
                scaled_part.reshape(group, rows, width),
            ],
            axis=1,
        ).astype(bf16),
        "cp",
        scatter_dimension=0,
        tiled=False,
    ).astype(f32)
    block_output = (
        block_input.astype(f32)
        + sums[:rows]
        + proj_offset.astype(f32)
        + down_offset.astype(f32)
    ).astype(bf16)
    scaled = sums[rows:]
    own_center = block_input.astype(f32)
    own_center = own_center - jnp.mean(own_center, axis=-1, keepdims=True)
    own_inverse = lax.rsqrt(jnp.mean(own_center * own_center, axis=-1, keepdims=True) + EPSILON)
    own_normed = own_center * own_inverse
    input_grad = out_cotangent.astype(f32) + own_inverse * (
        scaled
        - jnp.mean(scaled, axis=-1, keepdims=True)
        - own_normed * jnp.mean(scaled * own_normed, axis=-1, keepdims=True)
    )

    qkv_bgrad_placed = lax.dynamic_update_slice_in_dim(
        jnp.zeros((3, group, own), f32), qkv_bgrad.reshape(3, 1, own), rank, axis=1
    ).reshape(group, qkv_cols)
    up_bgrad_placed = lax.dynamic_update_slice_in_dim(
        jnp.zeros((group, hidden), f32), up_bgrad[None], rank, axis=0
    )
    vectors = jnp.concatenate(
        [qkv_bgrad_placed, up_bgrad_placed]
        + [
            term.reshape(group, own)
            for term in (
                bias_sum,
                jnp.sum(attn_in_grad * normed, axis=0),
                jnp.sum(attn_in_grad, axis=0),
                jnp.sum(feed_in_grad * normed, axis=0),
                jnp.sum(feed_in_grad, axis=0),
            )
        ],
        axis=1,
    )
    vectors = lax.dynamic_index_in_dim(
        lax.psum(vectors, ("rep", "cp")), rank, 0, keepdims=False
    )
    cuts = [qkv_cols, qkv_cols + hidden] + [
        qkv_cols + hidden + i * own for i in range(1, 5)
    ]
    (qkvb_out, upb_out, bias_out, gain1_out, shift1_out, gain2_out, shift2_out) = jnp.split(
        vectors, cuts
    )

    wide = jnp.concatenate([qkv_grad, up_grad], axis=1).astype(bf16)
    wide = wide.reshape(group, reps, own // reps, part_cols).transpose(1, 0, 2, 3)
    tall = jnp.concatenate([proj_grad, down_grad], axis=0).astype(bf16)
    wide_flat = wide.reshape(reps, -1, width)
    tall_flat = tall.reshape(reps, -1, width)
    both = lax.psum_scatter(
        jnp.concatenate([wide_flat, tall_flat], axis=1), "rep", scatter_dimension=0, tiled=False
    )
    cut = wide_flat.shape[1]
    moved = lax.all_to_all(
        both[:cut].reshape(group, own // reps, part_cols), "cp", 0, 0
    ).reshape(cut, width)
    gathered = lax.all_gather(jnp.concatenate([moved, both[cut:]], axis=0), "rep", axis=0).astype(
        f32
    )
    wide_out = (
        gathered[:, :cut]
        .reshape(reps, group, own // reps, part_cols)
        .transpose(0, 2, 1, 3)
        .reshape(own, group, part_cols)
    )
    qkv_out = (
        wide_out[:, :, :qkv_cols]
        .reshape(own, group, 3, own)
        .transpose(0, 2, 1, 3)
        .reshape(own, group * qkv_cols)
    )
    up_out = wide_out[:, :, qkv_cols:].reshape(own, group * hidden)
    tall_out = gathered[:, cut:].reshape(-1, width)
    return (
        block_output,
        input_grad,
        qkv_out,
        qkvb_out,
        tall_out[:own],
        bias_out,
        up_out,
        upb_out,
        tall_out[own:],
        bias_out,
        gain1_out,
        shift1_out,
        gain2_out,
        shift2_out,
    )


def solution(mesh):
    return jax.shard_map(
        body,
        mesh=mesh,
        in_specs=(
            P(("rep", "cp"), None),
            P("cp", None),
            P("cp"),
            P("cp", None),
            P("cp"),
            P("cp", None),
            P("cp"),
            P("cp", None),
            P("cp"),
            P("cp"),
            P("cp"),
            P("cp"),
            P("cp"),
            P(("rep", "cp"), None),
        ),
        out_specs=(
            P(("rep", "cp"), None),
            P(("rep", "cp"), None),
            P("cp", None),
            P("cp"),
            P("cp", None),
            P("cp"),
            P("cp", None),
            P("cp"),
            P("cp", None),
            P("cp"),
            P("cp"),
            P("cp"),
            P("cp"),
            P("cp"),
        ),
        check_vma=False,
    )
```

time: 1050 us -> 291 us (0.28)
  waiting for transfers between devices: 855 us -> 101 us
  local copies, waits for them, and re-layouts: 21.5 us -> 68.1 us
  blocking collectives: 97.1 us -> 58.4 us
  matrix products: 48.5 us -> 21.3 us
  other arithmetic: 6.6 us -> 18.4 us
    reduce_scatter x6 -> x2, waiting for transfers between devices: 562 us -> 64.4 us  [the longest x1 39.5 us: body(): lax.psum_scatter(jnp.concatenate([wide_flat, tall_flat], axis=1), 'rep',...]
    all_gather x4 -> x3, waiting for transfers between devices: 226 us -> 30.1 us  [the longest x1 20.8 us: body(): weights = lax.all_gather(mine, 'rep', axis=0)]
    psum x1 -> x0, waiting for transfers between devices: 64.5 us -> none  [body(): lax.psum((owned_qkv, owned_qkvb, owned_proj, owned_projb, owned_up, owned...]
    all_gather x3 -> x0, blocking collectives: 44.6 us -> none  [the longest x1 17.2 us: body(): lax.all_gather(keys_own, 'cp', axis=0, tiled=True)]
    unnamed x2 -> x0, blocking collectives: 27.7 us -> none
    dot_general x19 -> x18, matrix products: 48.5 us -> 21.3 us  [the longest x1 2.49 us: body(): feed_in_grad = jnp.dot(pre_low, up_matrix.T, preferred_element_type=f32)]
    reshape x0 -> x16, local copies, waits for them, and re-layouts: none -> 21.8 us  [the longest x1 6.3 us: body(): wide_out = gathered[:, :cut].reshape(reps, group, own // reps, part_cols)...]
    all_to_all x0 -> x1, blocking collectives: none -> 20.1 us  [body(): mine = lax.all_to_all(mine.transpose(1, 0, 2), 'cp', 0, 0)]
  transfers between devices with their start and end apart: 11 -> 6, of which waited for: 11 -> 5; matrix products, arithmetic and copies ran while one was open for 5% -> 14% of each run, Pallas kernels for 0% -> 0%
where the time goes in v1:
time: 291 us; the launch traced here: 287 us
  waiting for transfers between devices  101 us (35%)
  local copies, waits for them, and re-layouts  68.1 us (23%)
  blocking collectives  58.4 us (20%)
  matrix products  21.3 us (7%)
  other arithmetic  18.4 us (6%)
  between operations  14.5 us (5%)
  starting transfers between devices  5.03 us (2%)
    reduce_scatter x1, waiting for transfers between devices, body(): lax.psum_scatter(jnp.concatenate([wide_flat, tall_flat], axis=1), 'rep',...  39.5 us
    psum x1, blocking collectives, body(): lax.psum(vectors, ('rep', 'cp'))  38.3 us
    reduce_scatter x1, waiting for transfers between devices, body(): lax.psum_scatter(jnp.concatenate([branch_part.reshape(group, rows, width)...  24.9 us
    all_gather x1, waiting for transfers between devices, body(): weights = lax.all_gather(mine, 'rep', axis=0)  20.8 us
    all_to_all x1, blocking collectives, body(): mine = lax.all_to_all(mine.transpose(1, 0, 2), 'cp', 0, 0)  20.1 us
    all_gather x1, waiting for transfers between devices, body(): lax.all_gather(jnp.concatenate([block_input, out_cotangent, small_block],...  9.22 us
    unnamed x78, local copies, waits for them, and re-layouts  7.51 us
    all_to_all x1, waiting for transfers between devices, body(): lax.all_to_all(both[:cut].reshape(group, own // reps, part_cols), 'cp', 0...  6.43 us
  transfers between devices with their start and end apart: 6, of which 5 were waited for; matrix products, arithmetic and copies ran while one was open for 14% of the time, Pallas kernels for 0%

profile of v1, /device:TPU:11, one launch (start us, length us, event | category | flops | bytes accessed | tf_op | source)
XLA Modules:
  0.0 286.7 jit_solution(9439585052707011167)
XLA Ops:
  7.3 4.9 %concatenate.71 = bf16[1728]{0:T(1024)(128)(2,1)S(1)} concatenate(bf16[576]{0:T(1024)(128)(2,1)} %param.16, bf16[192]{0:T(256)(128)(2,1)} %param.18, bf16[192]{0:T(256)(128)(2,1)} %param.22, bf16[192]{0:T(256)(128)(2,1)} %param.23, bf16[192]{0:T(256)(128)(2,1)} %param.24, bf16[192]{0:T(256)(128)(2,1)} %param.25, bf16[192]{0:T(256)(128)(2,1)} %param.26), dimensions={0} | concatenate | bytes 6912 | tf_op jit(solution)/shard_map/concatenate | solution.py:96
  12.2 1.8 maximum_bitcast_fusion.1
  14.1 2.1 reshape.300
  16.2 1.9 copy.108
  18.1 2.3 concatenate.73
  20.3 2.7 concatenate.74
  23.2 1.0 fusion.32
  24.2 20.1 %all_to_all.10 = bf16[4,24,1344]{2,1,0:T(8,128)(2,1)} all-to-all(bf16[4,24,1344]{2,1,0:T(8,128)(2,1)S(1)} %fusion.32), channel_id=1, replica_groups=mesh['rep'=8,'cp'=4] {'cp'}, dimensions={0} | all-to-all | bytes 516096 | tf_op jit(solution)/shard_map/all_to_all | solution.py:126
  46.0 0.8 iota_compare_fusion
  46.8 9.2 %all-gather.12.cloned.1.call-done = bf16[4,259,768]{2,1,0:T(8,128)(2,1)} async-done(((bf16[1,259,768]{2,1,0:T(8,128)(2,1)}), bf16[4,259,768]{2,1,0:T(8,128)(2,1)}) %all-gather.12.cloned.1.call-update) | async-done | bytes 1591312 | tf_op jit(solution)/shard_map/all_gather | solution.py:103
  56.0 0.8 slice_bitcast_fusion.3
  58.1 1.3 convert_reduce_fusion
  59.4 1.5 multiply_reduce_fusion.2
  60.9 1.6 add_convert_fusion.3
  62.5 1.2 copy.89
  63.7 1.2 copy.90
  64.9 1.2 slice.213
  66.2 1.1 convolution_convert_fusion.5
  67.2 20.8 %all-gather.8.cloned.1.call-done = bf16[32,24,1344]{2,1,0:T(8,128)(2,1)} async-done(((bf16[4,24,1344]{2,1,0:T(8,128)(2,1)}), bf16[32,24,1344]{2,1,0:T(8,128)(2,1)}) %all-gather.8.cloned.1.call-update) | async-done | bytes 2064400 | tf_op jit(solution)/shard_map/all_gather | solution.py:127
  88.1 1.8 copy.83
  89.9 0.7 convolution_add_fusion.1
  91.6 0.8 fusion.1
  92.4 0.7 exponential_reduce_fusion
  93.3 1.0 multiply_reduce_fusion.3
  94.3 1.3 multiply_convert_fusion
  96.7 1.0 fusion.44
  97.7 1.9 multiply_convert_fusion.1
  99.8 1.7 fusion.51
  101.5 0.8 convolution_convert_fusion.1
  102.9 0.8 convolution_convert_fusion.2
  103.8 0.9 maximum_bitcast_fusion
  104.9 4.0 %reshape.312 = bf16[8,168,768]{2,1,0:T(8,128)(2,1)} reshape(bf16[8,4,24,1344]{3,2,1,0:T(8,128)(2,1)S(1)} %copy.91) | data formatting | bytes 4128768 | tf_op jit(solution)/shard_map/reshape | solution.py:266
  108.9 1.5 convolution_convert_fusion.3
  110.3 2.2 convolution_convert_fusion
  112.7 1.5 copy-done.2
  114.1 2.0 pad_maximum_fusion
  116.2 1.5 fusion.52
  118.1 0.8 fusion.11
  119.2 0.8 add_convert_fusion.1
  120.4 2.5 multiply_reduce_fusion
  122.9 1.2 pad_maximum_fusion.1
  124.1 39.5 %reduce-scatter.5.cloned.1.call-done = bf16[1,288,768]{2,1,0:T(8,128)(2,1)} async-done(((bf16[8,288,768]{2,1,0:T(8,128)(2,1)}), bf16[1,288,768]{2,1,0:T(8,128)(2,1)}) %reduce-scatter.5.cloned.1.call-update) | async-done | bytes 442384 | tf_op jit(solution)/shard_map/reduce_scatter | solution.py:268
  163.7 1.0 slice.226
  164.6 1.1 reshape.313
  165.8 4.7 %all-to-all-start.1 = ((bf16[4,24,1344]{2,1,0:T(8,128)(2,1)}), bf16[4,24,1344]{2,1,0:T(8,128)(2,1)S(1)}, u32[]{:S(2)}, u32[]{:S(2)}) async-start(bf16[4,24,1344]{2,1,0:T(8,128)(2,1)} %reshape.313), calls=%async_computation.3 | async-start | bytes 540672 | tf_op jit(solution)/shard_map/all_to_all | solution.py:272
  170.5 0.9 slice_bitcast_fusion.2
  171.4 6.4 %all-to-all-done.1 = bf16[4,24,1344]{2,1,0:T(8,128)(2,1)S(1)} async-done(((bf16[4,24,1344]{2,1,0:T(8,128)(2,1)}), bf16[4,24,1344]{2,1,0:T(8,128)(2,1)S(1)}, u32[]{:S(2)}, u32[]{:S(2)}) %all-to-all-start.1) | async-done | bytes 258080 | tf_op jit(solution)/shard_map/all_to_all | solution.py:272
  178.3 0.8 pad_maximum_fusion.4
  180.4 24.9 %reduce-scatter.3.cloned.1.call-done = bf16[1,256,768]{2,1,0:T(8,128)(2,1)} async-done(((bf16[4,256,768]{2,1,0:T(8,128)(2,1)}), bf16[1,256,768]{2,1,0:T(8,128)(2,1)}) %reduce-scatter.3.cloned.1.call-update) | async-done | bytes 393232 | tf_op jit(solution)/shard_map/reduce_scatter | solution.py:204
  205.3 1.0 convert_element_type.200
  206.7 1.0 convert_add_fusion.1
  207.8 38.3 %psum.7 = f32[4,2304]{1,0:T(4,128)S(1)} all-reduce(f32[4,2304]{1,0:T(4,128)S(1)} %concatenate.92), channel_id=1, replica_groups=mesh['rep'=8,'cp'=4] {'rep','cp'}, use_global_device_ids=true, to_apply=%region_18.19 | all-reduce | flops 9216 | bytes 73728 | tf_op jit(solution)/shard_map/psum | solution.py:254
  247.5 0.7 dynamic-slice_reduce_fusion
  248.1 3.8 %slice.228 = f32[8,168,768]{2,1,0:T(8,128)} slice(bf16[8,288,768]{2,1,0:T(8,128)(2,1)} %bitcast.127), slice={[0:8], [0:168], [0:768]} | slice | bytes 8257536 | tf_op jit(solution)/shard_map/slice | solution.py:279
  252.0 6.3 %reshape.315 = f32[8,4,24,1344]{3,2,1,0:T(8,128)} reshape(f32[8,168,768]{2,1,0:T(8,128)} %slice.228) | data formatting | bytes 8257536 | tf_op jit(solution)/shard_map/reshape | solution.py:280
  258.3 2.5 copy.92
  260.8 1.4 slice.229
  262.9 1.3 copy-done.1
  264.4 1.6 slice.233
  266.0 0.9 slice.231
  266.9 3.0 %copy.93 = f32[192,4,576]{0,2,1:T(8,128)} copy(f32[192,4,576]{2,0,1:T(8,128)} %slice.229) | data formatting | bytes 3538944 | tf_op jit(solution)/shard_map/slice | solution.py:285
  269.9 4.4 %copy.94 = f32[192,3,4,192]{3,2,1,0:T(4,128)} copy(f32[192,3,4,192]{0,3,1,2:T(8,128)} %bitcast.131) | data formatting | bytes 3538944 | tf_op jit(solution)/shard_map/transpose | solution.py:287
  274.3 3.7 %reshape.318 = f32[192,2304]{1,0:T(8,128)} reshape(f32[192,3,4,192]{3,2,1,0:T(4,128)} %copy.94) | data formatting | bytes 3538944 | tf_op jit(solution)/shard_map/reshape | solution.py:288
  277.9 1.7 copy.103
  (152 shorter events, 12.3 us)
Async XLA Ops:
  7.2 92.6 %copy-start = (bf16[768,768]{1,0:T(8,128)(2,1)S(1)}, bf16[768,768]{1,0:T(8,128)(2,1)}, u32[]{:S(2)}) copy-start(bf16[768,768]{1,0:T(8,128)(2,1)} %param.21) | copy-start | bytes 3538948
  7.2 6.9 %copy-start.15 = (bf16[192,2304]{1,0:T(8,128)(2,1)S(1)}, bf16[192,2304]{1,0:T(8,128)(2,1)}, u32[]{:S(2)}) copy-start(bf16[192,2304]{1,0:T(8,128)(2,1)} %param.15) | copy-start | bytes 2654212
  7.2 48.8 %all-gather.12.cloned.1.call-start = ((), (), s32[]{:S(2)}) async-start(), calls=%async_computation.8 | async-start | bytes 2027520 | tf_op jit(solution)/shard_map/all_gather | solution.py:103
  14.0 74.1 %all-gather.8.cloned.1.call-start = ((), (), s32[]{:S(2)}) async-start(), calls=%async_computation.6 | async-start | bytes 2433024 | tf_op jit(solution)/shard_map/all_gather | solution.py:127
  23.2 21.4 %copy-start.33 = (bf16[768]{0:T(1024)(128)(2,1)S(1)}, bf16[768]{0:T(1024)(128)(2,1)}, u32[]{:S(2)}) copy-start(bf16[768]{0:T(1024)(128)(2,1)} %param.20) | copy-start | bytes 4612
  44.4 119.3 %reduce-scatter.5.cloned.1.call-start = ((), (), s32[]{:S(2)}) async-start(), calls=%async_computation.5 | async-start | bytes 3981312 | tf_op jit(solution)/shard_map/reduce_scatter | solution.py:268
  59.4 3.2 %copy-start.25 = (f32[512]{0:T(512)}, f32[512]{0:T(512)S(1)}, u32[]{:S(2)}) copy-start(f32[512]{0:T(512)S(1)} %get-tuple-element.67) | copy-start | bytes 6148
  60.9 2.8 copy-start.27
  64.9 1.2 copy-start.13
  66.1 33.6 %copy-start.3 = (bf16[4,128,768]{2,1,0:T(8,128)(2,1)}, bf16[4,128,768]{2,1,0:T(8,128)(2,1)S(1)}, u32[]{:S(2)}) copy-start(bf16[4,128,768]{2,1,0:T(8,128)(2,1)S(1)} %slice.213) | copy-start | bytes 2359300
  88.1 1.8 copy-start.31
  89.9 7.8 %copy-start.5 = (bf16[4,8,24,1344]{3,2,1,0:T(8,128)(2,1)}, bf16[4,8,24,1344]{3,2,1,0:T(8,128)(2,1)S(1)}, u32[]{:S(2)}) copy-start(bf16[4,8,24,1344]{3,2,1,0:T(8,128)(2,1)S(1)} %copy.83) | copy-start | bytes 6193156
  90.6 0.8 copy-start.22
  90.6 0.8 copy-start.23
  90.6 1.0 copy-start.14
  92.4 0.9 copy-start.24
  96.7 1.0 copy-start.30
  97.7 4.8 %copy-start.19 = (f32[3,64,512]{2,1,0:T(8,128)}, f32[3,64,512]{2,1,0:T(8,128)S(1)}, u32[]{:S(2)}) copy-start(f32[3,64,512]{2,1,0:T(8,128)S(1)} %fusion.44) | copy-start | bytes 1179652
  99.7 2.7 copy-start.7
  99.8 2.6 copy-start.10
  99.8 1.7 copy-start.17
  101.5 0.9 copy-start.35
  101.5 1.4 copy-start.16
  112.5 1.6 copy-start.2
  116.1 1.7 copy-start.6
  116.1 89.1 %reduce-scatter.3.cloned.1.call-start = ((), (), s32[]{:S(2)}) async-start(), calls=%async_computation.4 | async-start | bytes 1966080 | tf_op jit(solution)/shard_map/reduce_scatter | solution.py:204
  116.2 1.7 copy-start.8
  116.2 1.8 copy-start.11
  116.2 1.9 copy-start.20
  118.1 1.1 copy-start.34
  119.2 0.8 copy-start.26
  119.2 0.8 copy-start.28
  119.2 1.1 copy-start.36
  164.6 14.5 %copy-start.4 = (bf16[128,768]{1,0:T(8,128)(2,1)S(1)}, bf16[128,768]{1,0:T(8,128)(2,1)}, u32[]{:S(2)}) copy-start(bf16[128,768]{1,0:T(8,128)(2,1)} %param.14) | copy-start | bytes 589828
  165.8 13.8 %copy-start.9 = (f32[512,3,64]{0,2,1:T(8,128)S(1)}, f32[512,3,64]{0,2,1:T(8,128)}, u32[]{:S(2)}) copy-start(f32[512,3,64]{0,2,1:T(8,128)} %copy-done.7) | copy-start | bytes 1179652
  165.8 13.8 %copy-start.12 = (f32[512,3,64]{0,2,1:T(8,128)S(1)}, f32[512,3,64]{0,2,1:T(8,128)}, u32[]{:S(2)}) copy-start(f32[512,3,64]{0,2,1:T(8,128)} %copy-done.10) | copy-start | bytes 1179652
  165.8 13.8 %copy-start.21 = (f32[3,64,512]{2,1,0:T(8,128)S(1)}, f32[3,64,512]{2,1,0:T(8,128)}, u32[]{:S(2)}) copy-start(f32[3,64,512]{2,1,0:T(8,128)} %copy-done.19) | copy-start | bytes 1179652
  165.8 12.1 %all-to-all-start.1 = ((bf16[4,24,1344]{2,1,0:T(8,128)(2,1)}), bf16[4,24,1344]{2,1,0:T(8,128)(2,1)S(1)}, u32[]{:S(2)}, u32[]{:S(2)}) async-start(bf16[4,24,1344]{2,1,0:T(8,128)(2,1)} %reshape.313), calls=%async_computation.3 | async-start | bytes 540672 | tf_op jit(solution)/shard_map/all_to_all | solution.py:272
  170.5 77.7 %all-gather.10.cloned.1.call-start = ((), (), s32[]{:S(2)}) async-start(), calls=%async_computation.7 | async-start | bytes 3981312 | tf_op jit(solution)/shard_map/all_gather | solution.py:275
  178.3 2.1 copy-start.29
  179.6 27.1 %copy-start.18 = (bf16[128,768]{1,0:T(8,128)(2,1)S(1)}, bf16[128,768]{1,0:T(8,128)(2,1)}, u32[]{:S(2)}) copy-start(bf16[128,768]{1,0:T(8,128)(2,1)} %param.27) | copy-start | bytes 589828
  246.9 32.8 %copy-start.32 = (f32[1,192]{1,0:T(1,128)}, f32[1,192]{1,0:T(1,128)S(1)}, u32[]{:S(2)}) copy-start(f32[1,192]{1,0:T(1,128)S(1)} %get-tuple-element.54) | copy-start | bytes 2308
  262.2 2.0 copy-start.1
Sparse Core Ops, SparseCore 0:
  14.1 41.8 all-gather.11
  57.9 30.1 all-gather.7
  116.3 47.3 reduce-scatter.4
  166.4 38.8 reduce-scatter.2
  207.6 32.4 all-gather.9

commit v2 on v1

--- a/solution.py
+++ b/solution.py
@@ -1,6 +1,10 @@
+import functools
+
 import jax
 import jax.numpy as jnp
 from jax import lax
+from jax.experimental import pallas as pl
+from jax.experimental.pallas import tpu as pltpu
 from jax.sharding import PartitionSpec as P
 
 HEAD = 64
@@ -62,6 +66,406 @@
         0.5 * (1.0 + lax.erf(preact * ROOT_HALF))
         + preact * jnp.exp(-0.5 * preact * preact) * INV_ROOT_TWO_PI
     )
+
+SPLIT = 8
+BITS = 3
+
+
+def rep_bit(r, k):
+    return (r // (1 << k)) % 2
+
+
+def rep_partner(r, k):
+    return r + (1 << k) * (1 - 2 * rep_bit(r, k))
+
+
+def greet(group, reps, z, r, rep_bits):
+    barrier = pltpu.get_barrier_semaphore()
+    for t in range(1, group):
+        pl.semaphore_signal(barrier, inc=1, device_id={"cp": (z + t) % group})
+    for k in range(rep_bits):
+        pl.semaphore_signal(barrier, inc=1, device_id={"rep": rep_partner(r, k)})
+    pl.semaphore_wait(barrier, group - 1 + rep_bits)
+
+
+def remote(src, dst, send, recv, device):
+    return pltpu.make_async_remote_copy(
+        src_ref=src, dst_ref=dst, send_sem=send, recv_sem=recv, device_id=device
+    )
+
+
+HALF_BITS = ((1, 2), (2, 1))
+
+
+def gather_kernel(
+    group, reps,
+    x_ref, c_ref, s_ref, pu_ref, pq_ref,
+    xa_ref, ca_ref, sa_ref, cu_ref, cq_ref,
+    loc_sem, line_send, line_recv, small_send, small_recv, z_send, z_recv, g_send, g_recv,
+):
+    z = lax.axis_index("cp")
+    r = lax.axis_index("rep")
+    greet(group, reps, z, r, BITS)
+    core = rep_bit(r, 0)
+    pieces = (pu_ref, pq_ref)
+    full = (cu_ref, cq_ref)
+
+    def own(h):
+        d1, d2 = HALF_BITS[h]
+        return full[h].at[core, rep_bit(r, d1), rep_bit(r, d2)]
+
+    waits = []
+    for h in range(2):
+        for t in range(1, group):
+            to = (z + t) % group
+            copy = remote(
+                pieces[h].at[to], own(h).at[z], z_send.at[h, t], z_recv.at[h, t], {"cp": to}
+            )
+            copy.start()
+            waits.append(copy)
+    for t in range(1, group):
+        copy = remote(
+            s_ref, sa_ref.at[z], small_send.at[t], small_recv.at[t], {"cp": (z + t) % group}
+        )
+        copy.start()
+        waits.append(copy)
+    lines = ((x_ref, xa_ref), (c_ref, ca_ref))
+
+    def line_copy(i, source, direction, first):
+        src = lines[i][0] if first else lines[i][1].at[source]
+        return remote(
+            src,
+            lines[i][1].at[source],
+            line_send.at[i, direction, source],
+            line_recv.at[i, source],
+            {"cp": z + 1 - 2 * direction},
+        )
+
+    for i in range(2):
+        @pl.when(z < group - 1)
+        def _():
+            line_copy(i, z, 0, True).start()
+
+        @pl.when(z > 0)
+        def _():
+            line_copy(i, z, 1, True).start()
+    locals_ = [
+        pltpu.make_async_copy(x_ref, xa_ref.at[z], loc_sem.at[0]),
+        pltpu.make_async_copy(c_ref, ca_ref.at[z], loc_sem.at[1]),
+        pltpu.make_async_copy(s_ref, sa_ref.at[z], loc_sem.at[2]),
+        pltpu.make_async_copy(pu_ref.at[z], own(0).at[z], loc_sem.at[3]),
+        pltpu.make_async_copy(pq_ref.at[z], own(1).at[z], loc_sem.at[4]),
+    ]
+    for copy in locals_:
+        copy.start()
+    for copy in locals_:
+        copy.wait()
+
+    for copy in waits:
+        copy.wait()
+
+    def stage_copy(h, stage):
+        d1, d2 = HALF_BITS[h]
+        if stage == 0:
+            ref, bit = own(h), d2
+        elif stage == 1:
+            ref, bit = full[h].at[core, rep_bit(r, d1)], d1
+        else:
+            ref, bit = full[h].at[core], 0
+        return remote(
+            ref, ref, g_send.at[h, stage], g_recv.at[h, stage], {"rep": rep_partner(r, bit)}
+        )
+
+    def step(t):
+        for i in range(2):
+            @pl.when(z >= t)
+            def _():
+                line_copy(i, z - t, 0, False).wait_recv()
+
+                @pl.when(z < group - 1)
+                def _():
+                    line_copy(i, z - t, 0, False).start()
+
+            @pl.when(z + t < group)
+            def _():
+                line_copy(i, z + t, 1, False).wait_recv()
+
+                @pl.when(z > 0)
+                def _():
+                    line_copy(i, z + t, 1, False).start()
+
+    stages = [[stage_copy(h, s) for h in range(2)] for s in range(BITS)]
+    for copy in stages[0]:
+        copy.start()
+    for s in range(BITS):
+        for copy in stages[s]:
+            copy.wait()
+        if s + 1 < BITS:
+            for copy in stages[s + 1]:
+                copy.start()
+        if s + 1 < group:
+            step(s + 1)
+    for t in range(BITS + 1, group):
+        step(t)
+    for i in range(2):
+        for t in range(group):
+            @pl.when((z >= t) & (z < group - 1))
+            def _():
+                line_copy(i, z - t, 0, t == 0).wait_send()
+
+            @pl.when((z + t < group) & (z > 0))
+            def _():
+                line_copy(i, z + t, 1, t == 0).wait_send()
+
+
+def reduce_kernel(
+    group, reps, rep_bits,
+    qkv_ref, up_ref, proj_ref, down_ref, vec_ref, parts_ref, x_ref, c_ref, bias_ref,
+    y_ref, dx_ref, qkv_out, proj_out, up_out, down_out, vec_out,
+    buf_a, buf_b, r0_a, r0_b, r1_a, r1_b, r2_a, r2_b, up_send_a, up_send_b, ru_a, ru_b,
+    zr_a, zr_b, full_a, full_b, vs, vr, vz, sr,
+    rs_send, rs_recv, u_send, u_recv, z_send, z_recv, g_send, g_recv,
+    v_send, v_recv, vz_send, vz_recv, s_send, s_recv,
+):
+    f32, bf16 = jnp.float32, jnp.bfloat16
+    z = lax.axis_index("cp")
+    r = lax.axis_index("rep")
+    greet(group, reps, z, r, rep_bits)
+    core = rep_bit(r, 0)
+    rows = x_ref.shape[0]
+    own, width = proj_ref.shape
+    unit = own // SPLIT
+    hidden = up_ref.shape[1]
+    qkv_cols = qkv_ref.shape[1]
+    half_w = buf_a.shape[-1]
+    cut = half_w - hidden
+    buf = (buf_a, buf_b)
+    r0 = (r0_a, r0_b)
+    r1 = (r1_a, r1_b)
+    r2 = (r2_a, r2_b)
+    up_send = (up_send_a, up_send_b)
+    ru = (ru_a, ru_b)
+    zr = (zr_a, zr_b)
+    full = (full_a, full_b)
+    zw = (zr_a.shape[-1], zr_b.shape[-1])
+
+    sums = []
+    for t in range(1, group):
+        to = (z + t) % group
+        copy = remote(parts_ref.at[to], sr.at[t - 1], s_send.at[t], s_recv.at[t], {"cp": to})
+        sums.append(copy)
+
+    def fill(s, core_bit):
+        first, second = s // 2, s % 2
+        base = (core_bit * 4 + s) * unit
+        proj = proj_ref[pl.ds(pl.multiple_of(base, 8), unit), :].astype(bf16)
+        for u in range(group):
+            at = pl.ds(pl.multiple_of(u * own + base, 8), unit)
+            down = down_ref[at, :].astype(bf16)
+            buf_a[core_bit, first, second, u] = jnp.concatenate(
+                [up_ref[at, :].astype(bf16), down[:, :cut]], axis=1
+            )
+            buf_b[core_bit, second, first, u] = jnp.concatenate(
+                [
+                    qkv_ref[at, :].astype(bf16),
+                    proj[:, u * (width // group) : (u + 1) * (width // group)],
+                    down[:, cut:],
+                ],
+                axis=1,
+            )
+
+    def fill_loop(core_bit):
+        lax.fori_loop(0, 4, lambda s, n: (fill(s, core_bit), n)[1], 0)
+
+    def rs_copy(h, stage):
+        d1, d2 = HALF_BITS[h]
+        if stage == 0:
+            src, dst, bit = buf[h].at[1 - core], r0[h], 0
+        elif stage == 1:
+            src, dst, bit = r0[h].at[1 - rep_bit(r, d1)], r1[h], d1
+        else:
+            src, dst, bit = r1[h].at[1 - rep_bit(r, d2)], r2[h], d2
+        return remote(
+            src, dst, rs_send.at[h, stage], rs_recv.at[h, stage], {"rep": rep_partner(r, bit)}
+        )
+
+    def v_copy(k):
+        return remote(
+            vs.at[k], vr.at[k], v_send.at[k], v_recv.at[k], {"rep": rep_partner(r, k)}
+        )
+
+    fill_loop(1 - core)
+    rs = [[rs_copy(h, s) for h in range(2)] for s in range(BITS)]
+    for copy in rs[0]:
+        copy.start()
+    vs[0] = vec_ref[...]
+    v_copy(0).start()
+    for copy in sums:
+        copy.start()
+    fill_loop(core)
+
+    for h in range(2):
+        rs[0][h].wait()
+
+        def add0(n, carry):
+            a, b, u = n // (2 * group), (n // group) % 2, n % group
+            r0[h][a, b, u] = (
+                r0[h][a, b, u].astype(f32) + buf[h][core, a, b, u].astype(f32)
+            ).astype(bf16)
+            return carry
+
+        lax.fori_loop(0, 4 * group, add0, 0)
+        rs[1][h].start()
+    v_copy(0).wait()
+    vs[1] = vs[0] + vr[0]
+    v_copy(1).start()
+    for h in range(2):
+        rs[1][h].wait()
+        mine = rep_bit(r, HALF_BITS[h][0])
+
+        def add1(n, carry):
+            b, u = n // group, n % group
+            r1[h][b, u] = (
+                r1[h][b, u].astype(f32) + r0[h][mine, b, u].astype(f32)
+            ).astype(bf16)
+            return carry
+
+        lax.fori_loop(0, 2 * group, add1, 0)
+        rs[2][h].start()
+    v_copy(1).wait()
+    vs[2] = vs[1] + vr[1]
+    v_copy(2).start()
+    for h in range(2):
+        rs[2][h].wait()
+        mine = rep_bit(r, HALF_BITS[h][1])
+        for u in range(group):
+            up_send[h][0, u] = (
+                r2[h][u].astype(f32) + r1[h][mine, u].astype(f32)
+            ).astype(bf16)
+    v_copy(2).wait()
+    vs[3] = vs[2] + vr[2]
+    for k in range(BITS, rep_bits):
+        copies = [
+            remote(
+                up_send[h].at[k - BITS],
+                ru[h].at[k - BITS],
+                u_send.at[h, k - BITS],
+                u_recv.at[h, k - BITS],
+                {"rep": rep_partner(r, k)},
+            )
+            for h in range(2)
+        ] + [v_copy(k)]
+        for copy in copies:
+            copy.start()
+        for copy in copies:
+            copy.wait()
+        for h in range(2):
+            up_send[h][k - BITS + 1] = (
+                up_send[h][k - BITS].astype(f32) + ru[h][k - BITS].astype(f32)
+            ).astype(bf16)
+        vs[k + 1] = vs[k] + vr[k]
+    last = rep_bits - BITS
+    final = [up_send[h].at[last] for h in range(2)]
+    exchange = []
+    for t in range(1, group):
+        to = (z + t) % group
+        for h in range(2):
+            exchange.append(
+                remote(
+                    final[h].at[to, :, pl.ds(0, zw[h])],
+                    zr[h].at[t - 1],
+                    z_send.at[h, t],
+                    z_recv.at[h, t],
+                    {"cp": to},
+                )
+            )
+        exchange.append(
+            remote(
+                vs.at[rep_bits, to], vz.at[t - 1], vz_send.at[t], vz_recv.at[t], {"cp": to}
+            )
+        )
+    for copy in exchange:
+        copy.start()
+
+    def mine_of(h):
+        d1, d2 = HALF_BITS[h]
+        return full[h].at[core, rep_bit(r, d1), rep_bit(r, d2)]
+
+    for copy in exchange:
+        copy.wait()
+    used = (hidden, qkv_cols)
+    for h in range(2):
+        piece = mine_of(h)
+        for u in range(group):
+            piece[u, :, used[h] :] = final[h][u, :, used[h] :]
+        piece[z, :, : used[h]] = final[h][z, :, : used[h]]
+        for t in range(1, group):
+            piece[(z + group - t) % group, :, : used[h]] = zr[h][t - 1][:, : used[h]]
+    total = vs[rep_bits, z]
+    for t in range(1, group):
+        total = total + vz[t - 1]
+    vec_out[...] = total
+
+    def g_copy(h, stage):
+        d1, d2 = HALF_BITS[h]
+        if stage == 0:
+            ref, bit = mine_of(h), d2
+        elif stage == 1:
+            ref, bit = full[h].at[core, rep_bit(r, d1)], d1
+        else:
+            ref, bit = full[h].at[core], 0
+        return remote(
+            ref, ref, g_send.at[h, stage], g_recv.at[h, stage], {"rep": rep_partner(r, bit)}
+        )
+
+    gather = [[g_copy(h, s) for h in range(2)] for s in range(BITS)]
+    for copy in gather[0]:
+        copy.start()
+    for copy in sums:
+        copy.wait()
+    xs = x_ref[...].astype(f32)
+    branch = xs + bias_ref[...]
+    scaled = parts_ref[z, rows:].astype(f32)
+    branch = branch + parts_ref[z, :rows].astype(f32)
+    for t in range(1, group):
+        branch = branch + sr[t - 1, :rows].astype(f32)
+        scaled = scaled + sr[t - 1, rows:].astype(f32)
+    y_ref[...] = branch.astype(bf16)
+    center = xs - jnp.mean(xs, axis=-1, keepdims=True)
+    inverse = lax.rsqrt(jnp.mean(center * center, axis=-1, keepdims=True) + EPSILON)
+    normed = center * inverse
+    dx_ref[...] = c_ref[...].astype(f32) + inverse * (
+        scaled
+        - jnp.mean(scaled, axis=-1, keepdims=True)
+        - normed * jnp.mean(scaled * normed, axis=-1, keepdims=True)
+    )
+    for s in range(BITS):
+        for h in range(2):
+            gather[s][h].wait()
+            if s + 1 < BITS:
+                gather[s + 1][h].start()
+
+    def write(s, carry):
+        c0, first, second = s // 4, (s // 2) % 2, s % 2
+        base = s * unit
+        at = pl.ds(pl.multiple_of(base, 8), unit)
+        for u in range(group):
+            a = full_a[c0, first, second, u].astype(f32)
+            b = full_b[c0, second, first, u].astype(f32)
+            up_out[at, u * hidden : (u + 1) * hidden] = a[:, :hidden]
+            rows_at = pl.ds(pl.multiple_of(u * own + base, 8), unit)
+            down_out[rows_at, :cut] = a[:, hidden:]
+            down_out[rows_at, cut:] = b[:, qkv_cols + width // group :]
+            proj_out[at, u * (width // group) : (u + 1) * (width // group)] = b[
+                :, qkv_cols : qkv_cols + width // group
+            ]
+            for j in range(3):
+                qkv_out[at, j * width + u * own : j * width + (u + 1) * own] = b[
+                    :, j * own : (j + 1) * own
+                ]
+        return carry
+
+    lax.fori_loop(0, SPLIT, write, 0)
 
 
 def body(
@@ -96,16 +500,52 @@
     small = jnp.concatenate(
         [qkv_bias, proj_bias, down_bias, attention_gain, attention_shift, feed_gain, feed_shift]
     )
-    small_rows = -(-small.shape[0] // width)
-    small_block = jnp.pad(small, (0, small_rows * width - small.shape[0])).reshape(
-        small_rows, width
-    )
-    packed = lax.all_gather(
-        jnp.concatenate([block_input, out_cotangent, small_block], axis=0), "cp", axis=0
-    )
-    tokens = packed[:, :rows].reshape(total_rows, width)
-    cotangent = packed[:, rows : 2 * rows].reshape(total_rows, width)
-    small_all = packed[:, 2 * rows :].reshape(group, small_rows * width)
+    small = jnp.pad(small, (0, -small.shape[0] % 128))[None]
+    unit = own // SPLIT
+    r = lax.axis_index("rep")
+    slot = rep_bit(r, 0) * 4 + rep_bit(r, 1) * 2 + rep_bit(r, 2)
+    up_piece = (
+        lax.dynamic_slice_in_dim(up_weight, slot * unit, unit, axis=0)
+        .reshape(unit, group, hidden)
+        .transpose(1, 0, 2)
+    )
+    qkv_piece = (
+        lax.dynamic_slice_in_dim(qkv_weight, slot * unit, unit, axis=0)
+        .reshape(unit, 3, group, own)
+        .transpose(2, 0, 1, 3)
+        .reshape(group, unit, qkv_cols)
+    )
+    vmem = pl.BlockSpec(memory_space=pltpu.VMEM)
+    dma = pltpu.SemaphoreType.DMA
+    tokens, cotangent, small_all, up_slices, qkv_slices = pl.pallas_call(
+        functools.partial(gather_kernel, group, reps),
+        out_shape=[
+            jax.ShapeDtypeStruct((group, rows, width), bf16),
+            jax.ShapeDtypeStruct((group, rows, width), bf16),
+            jax.ShapeDtypeStruct((group,) + small.shape, bf16),
+            jax.ShapeDtypeStruct((2, 2, 2) + up_piece.shape, bf16),
+            jax.ShapeDtypeStruct((2, 2, 2) + qkv_piece.shape, bf16),
+        ],
+        in_specs=[vmem] * 5,
+        out_specs=[vmem] * 5,
+        scratch_shapes=[
+            dma((5,)),
+            dma((2, 2, group)),
+            dma((2, group)),
+            dma((group,)),
+            dma((group,)),
+            dma((2, group)),
+            dma((2, group)),
+            dma((2, BITS)),
+            dma((2, BITS)),
+        ],
+        compiler_params=pltpu.CompilerParams(
+            collective_id=0, has_side_effects=True, vmem_limit_bytes=50 * 2**20
+        ),
+    )(block_input, out_cotangent, small, up_piece, qkv_piece)
+    tokens = tokens.reshape(total_rows, width)
+    cotangent = cotangent.reshape(total_rows, width)
+    small_all = small_all.reshape(group, -1)
     joined_offset_all = small_all[:, :qkv_cols].reshape(group * qkv_cols)
     joined_offset = lax.dynamic_slice_in_dim(
         joined_offset_all.reshape(3, group, own), rank, 1, axis=1
@@ -115,19 +555,8 @@
         for i in range(6)
     )
 
-    stripes = jnp.concatenate(
-        [
-            qkv_weight.reshape(own, 3, group, own).transpose(0, 2, 1, 3).reshape(own, group, -1),
-            up_weight.reshape(own, group, hidden),
-        ],
-        axis=2,
-    ).reshape(reps, own // reps, group, part_cols)
-    mine = lax.dynamic_index_in_dim(stripes, lax.axis_index("rep"), 0, keepdims=False)
-    mine = lax.all_to_all(mine.transpose(1, 0, 2), "cp", 0, 0)
-    weights = lax.all_gather(mine, "rep", axis=0)
-    weights = weights.transpose(1, 0, 2, 3).reshape(width, part_cols)
-    joined_matrix = weights[:, :qkv_cols]
-    up_matrix = weights[:, qkv_cols:]
+    up_matrix = up_slices.transpose(3, 0, 1, 2, 4, 5).reshape(width, hidden)
+    joined_matrix = qkv_slices.transpose(3, 0, 2, 1, 4, 5).reshape(width, qkv_cols)
 
     positions = jnp.arange(total_rows, dtype=jnp.int32)
     cos_table, sin_table = rotary_tables(positions)
@@ -201,34 +630,10 @@
     attn_in_grad = jnp.dot(joined_low, joined_matrix.T, preferred_element_type=f32)
 
     scaled_part = attn_in_grad * gain_one.astype(f32) + feed_in_grad * gain_two.astype(f32)
-    sums = lax.psum_scatter(
-        jnp.concatenate(
-            [
-                branch_part.reshape(group, rows, width),
-                scaled_part.reshape(group, rows, width),
-            ],
-            axis=1,
-        ).astype(bf16),
-        "cp",
-        scatter_dimension=0,
-        tiled=False,
-    ).astype(f32)
-    block_output = (
-        block_input.astype(f32)
-        + sums[:rows]
-        + proj_offset.astype(f32)
-        + down_offset.astype(f32)
+    parts = jnp.concatenate(
+        [branch_part.reshape(group, rows, width), scaled_part.reshape(group, rows, width)], axis=1
     ).astype(bf16)
-    scaled = sums[rows:]
-    own_center = block_input.astype(f32)
-    own_center = own_center - jnp.mean(own_center, axis=-1, keepdims=True)
-    own_inverse = lax.rsqrt(jnp.mean(own_center * own_center, axis=-1, keepdims=True) + EPSILON)
-    own_normed = own_center * own_inverse
-    input_grad = out_cotangent.astype(f32) + own_inverse * (
-        scaled
-        - jnp.mean(scaled, axis=-1, keepdims=True)
-        - own_normed * jnp.mean(scaled * own_normed, axis=-1, keepdims=True)
-    )
+    bias_row = (proj_offset.astype(f32) + down_offset.astype(f32))[None]
 
     qkv_bgrad_placed = lax.dynamic_update_slice_in_dim(
         jnp.zeros((3, group, own), f32), qkv_bgrad.reshape(3, 1, own), rank, axis=1
@@ -250,9 +655,72 @@
         ],
         axis=1,
     )
-    vectors = lax.dynamic_index_in_dim(
-        lax.psum(vectors, ("rep", "cp")), rank, 0, keepdims=False
-    )
+    rep_bits = reps.bit_length() - 1
+    half_w = (qkv_cols + own + width + hidden) // 2
+    piece = (group, unit, half_w)
+    halves = lambda *lead: [pltpu.VMEM(lead + piece, bf16)] * 2
+    spare = max(rep_bits - BITS, 1)
+    (block_output, input_grad, qkv_out, proj_out, up_out, down_out, vectors) = pl.pallas_call(
+        functools.partial(reduce_kernel, group, reps, rep_bits),
+        out_shape=[
+            jax.ShapeDtypeStruct((rows, width), bf16),
+            jax.ShapeDtypeStruct((rows, width), f32),
+            jax.ShapeDtypeStruct((own, group * qkv_cols), f32),
+            jax.ShapeDtypeStruct((own, width), f32),
+            jax.ShapeDtypeStruct((own, group * hidden), f32),
+            jax.ShapeDtypeStruct((hidden, width), f32),
+            jax.ShapeDtypeStruct((1, vectors.shape[1]), f32),
+        ],
+        in_specs=[vmem] * 9,
+        out_specs=[vmem] * 7,
+        scratch_shapes=(
+            halves(2, 2, 2)
+            + halves(2, 2)
+            + halves(2)
+            + halves()
+            + halves(rep_bits - BITS + 1)
+            + halves(spare)
+            + [
+                pltpu.VMEM((group - 1, unit, hidden), bf16),
+                pltpu.VMEM((group - 1, unit, -(-qkv_cols // 128) * 128), bf16),
+            ]
+            + halves(2, 2, 2)
+            + [
+                pltpu.VMEM((rep_bits + 1, group, 1, vectors.shape[1]), f32),
+                pltpu.VMEM((rep_bits, group, 1, vectors.shape[1]), f32),
+                pltpu.VMEM((group - 1, 1, vectors.shape[1]), f32),
+                pltpu.VMEM((group - 1, 2 * rows, width), bf16),
+                dma((2, BITS)),
+                dma((2, BITS)),
+                dma((2, spare)),
+                dma((2, spare)),
+                dma((2, group)),
+                dma((2, group)),
+                dma((2, BITS)),
+                dma((2, BITS)),
+                dma((rep_bits,)),
+                dma((rep_bits,)),
+                dma((group,)),
+                dma((group,)),
+                dma((group,)),
+                dma((group,)),
+            ]
+        ),
+        compiler_params=pltpu.CompilerParams(
+            collective_id=1, has_side_effects=True, vmem_limit_bytes=60 * 2**20
+        ),
+    )(
+        qkv_grad,
+        up_grad,
+        proj_grad,
+        down_grad,
+        vectors[:, None],
+        parts,
+        block_input,
+        out_cotangent,
+        bias_row,
+    )
+    vectors = vectors[0]
     cuts = [qkv_cols, qkv_cols + hidden] + [
         qkv_cols + hidden + i * own for i in range(1, 5)
     ]
@@ -260,45 +728,16 @@
         vectors, cuts
     )
 
-    wide = jnp.concatenate([qkv_grad, up_grad], axis=1).astype(bf16)
-    wide = wide.reshape(group, reps, own // reps, part_cols).transpose(1, 0, 2, 3)
-    tall = jnp.concatenate([proj_grad, down_grad], axis=0).astype(bf16)
-    wide_flat = wide.reshape(reps, -1, width)
-    tall_flat = tall.reshape(reps, -1, width)
-    both = lax.psum_scatter(
-        jnp.concatenate([wide_flat, tall_flat], axis=1), "rep", scatter_dimension=0, tiled=False
-    )
-    cut = wide_flat.shape[1]
-    moved = lax.all_to_all(
-        both[:cut].reshape(group, own // reps, part_cols), "cp", 0, 0
-    ).reshape(cut, width)
-    gathered = lax.all_gather(jnp.concatenate([moved, both[cut:]], axis=0), "rep", axis=0).astype(
-        f32
-    )
-    wide_out = (
-        gathered[:, :cut]
-        .reshape(reps, group, own // reps, part_cols)
-        .transpose(0, 2, 1, 3)
-        .reshape(own, group, part_cols)
-    )
-    qkv_out = (
-        wide_out[:, :, :qkv_cols]
-        .reshape(own, group, 3, own)
-        .transpose(0, 2, 1, 3)
-        .reshape(own, group * qkv_cols)
-    )
-    up_out = wide_out[:, :, qkv_cols:].reshape(own, group * hidden)
-    tall_out = gathered[:, cut:].reshape(-1, width)
     return (
         block_output,
         input_grad,
         qkv_out,
         qkvb_out,
-        tall_out[:own],
+        proj_out,
         bias_out,
         up_out,
         upb_out,
-        tall_out[own:],
+        down_out,
         bias_out,
         gain1_out,
         shift1_out,

time: 291 us -> 183 us (0.63)
  Pallas kernels: 0 us -> 106 us
  waiting for transfers between devices: 101 us -> 0 us
  blocking collectives: 58.4 us -> 0 us
  local copies, waits for them, and re-layouts: 68.1 us -> 38.6 us
  between operations: 14.5 us -> 1.33 us
  other arithmetic: 18.4 us -> 8.94 us
  starting transfers between devices: 5.03 us -> 0 us
  matrix products: 21.3 us -> 25.4 us
    pallas_call x0 -> x2, Pallas kernels: none -> 106 us  [the longest x1 72.8 us: body(): pl.pallas_call(functools.partial(reduce_kernel, group, reps, rep_bits), o...]
    reduce_scatter x2 -> x0, waiting for transfers between devices: 64.4 us -> none  [the longest x1 39.5 us: body(): lax.psum_scatter(jnp.concatenate([wide_flat, tall_flat], axis=1), 'rep',...]
    psum x1 -> x0, blocking collectives: 38.3 us -> none  [body(): lax.psum(vectors, ('rep', 'cp'))]
    all_gather x3 -> x0, waiting for transfers between devices: 30.1 us -> none  [the longest x1 20.8 us: body(): weights = lax.all_gather(mine, 'rep', axis=0)]
    reshape x9 -> x3, local copies, waits for them, and re-layouts: 21.2 us -> 0.34 us  [the longest x2 0.33 us: body(): qkv_piece = lax.dynamic_slice_in_dim(qkv_weight, slot * unit, unit, axis=...]
    all_to_all x1 -> x0, blocking collectives: 20.1 us -> none  [body(): mine = lax.all_to_all(mine.transpose(1, 0, 2), 'cp', 0, 0)]
    slice x10 -> x1, local copies, waits for them, and re-layouts: 14.1 us -> 0.05 us  [body(): joined_out[:, own:2 * own].reshape(total_rows, heads, HEAD)]
    transpose x4 -> x3, local copies, waits for them, and re-layouts: 8.88 us -> 1.2 us  [the longest x1 1.03 us: body(): qkv_slices.transpose(3, 0, 2, 1, 4, 5).reshape(width, qkv_cols)]
  transfers between devices with their start and end apart: 6 -> 0, of which waited for: 5 -> 0; matrix products, arithmetic and copies ran while one was open for 14% -> 0% of each run, Pallas kernels for 0% -> 0%
where the time goes in v2:
time: 183 us; the launch traced here: 180 us
  Pallas kernels  106 us (58%)
  local copies, waits for them, and re-layouts  38.6 us (21%)
  matrix products  25.4 us (14%)
  other arithmetic  8.94 us (5%)
    pallas_call x1, Pallas kernels, body(): pl.pallas_call(functools.partial(reduce_kernel, group, reps, rep_bits), o...  72.8 us
    pallas_call x1, Pallas kernels, body(): pl.pallas_call(functools.partial(gather_kernel, group, reps), out_shape=[...  33 us
    unnamed x88, local copies, waits for them, and re-layouts  14.7 us
    concatenate x1, local copies, waits for them, and re-layouts, body(): jnp.concatenate([qkv_bias, proj_bias, down_bias, attention_gain, attentio...  4.88 us
    split x3, local copies, waits for them, and re-layouts, body(): jnp.split(vectors, cuts)  4.03 us
    reshape x5, local copies, waits for them, and re-layouts, body(): term.reshape(group, own)  3.76 us

profile of v2, /device:TPU:11, one launch (start us, length us, event | category | flops | bytes accessed | tf_op | source)
XLA Modules:
  0.0 180.0 jit_solution(14171364241152856504)
XLA Ops:
  0.8 4.9 %concatenate.45 = bf16[1728]{0:T(1024)(128)(2,1)S(1)} concatenate(bf16[576]{0:T(1024)(128)(2,1)} %param.16, bf16[192]{0:T(256)(128)(2,1)} %param.18, bf16[192]{0:T(256)(128)(2,1)} %param.22, bf16[192]{0:T(256)(128)(2,1)} %param.23, bf16[192]{0:T(256)(128)(2,1)} %param.24, bf16[192]{0:T(256)(128)(2,1)} %param.25, bf16[192]{0:T(256)(128)(2,1)} %param.26), dimensions={0} | concatenate | bytes 6912 | tf_op jit(solution)/shard_map/concatenate | solution.py:500
  5.7 0.7 convert_element_type.191
  6.4 1.0 convert_reduce_fusion.1
  7.3 0.7 reshape.306
  8.2 0.9 constant_dynamic-slice_fusion
  9.5 0.9 constant_dynamic-slice_fusion.1
  10.5 0.8 iota_compare_fusion
  11.3 33.0 %shard_map.245 = (bf16[4,128,768]{2,1,0:T(8,128)(2,1)S(1)}, bf16[4,128,768]{2,1,0:T(8,128)(2,1)S(1)}, bf16[4,1,1792]{2,1,0:T(2,128)(2,1)S(1)}, bf16[2,2,2,4,24,7...) custom-call(bf16[128,768]{1,0:T(8,128)(2,1)S(1)} %copy-done.2, bf16[128,768]{1,0:T(8,128)(2,1)S(1)} %copy-done.1, ...), custom_call_target="tpu_custom_call" | custom-call | tf_op jit(solution)/shard_map/pallas_call | solution.py:520
  44.3 1.0 copy.36
  45.5 0.6 fusion.22
  46.0 0.4 multiply_reduce_fusion.2
  46.4 0.6 add_rsqrt_fusion
  47.1 0.7 add.162.bias_ref
  48.4 1.1 convolution_convert_fusion.1
  49.8 0.5 add_convert_fusion.2
  50.3 1.1 copy-done.14
  51.4 0.7 convolution_add_fusion.1
  52.1 0.7 slice.173
  52.8 0.7 slice.174
  53.5 0.7 slice.175
  54.2 0.7 fusion.18
  54.9 0.9 multiply_convert_fusion.1
  55.8 2.0 %fusion.37 = (f32[768]{0:T(1024)S(1)}, bf16[512,768]{1,0:T(8,128)(2,1)}) fusion(f32[512,768]{1,0:T(8,128)S(1)} %get-tuple-element.85, bf16[512,768]{1,0:T(8,128)(2,1)S(1)} %bitcast.88, bf16[768,768]{1,0:T(8,128)(2,1)S(1)} %copy-done), kind=kOutput, calls=%fused_computation.102 | convolution fusion | flops 608304384 | bytes 4328448 | tf_op jit(solution)/shard_map/dot_general | solution.py:600
  57.8 0.6 broadcast_in_dim.27
  58.4 0.9 dynamic_update_slice.7
  59.3 2.3 %fusion.10 = f32[512,768]{1,0:T(8,128)S(1)} fusion(bf16[768,768]{1,0:T(8,128)(2,1)} %bitcast.109, bf16[512,768]{1,0:T(8,128)(2,1)} %get-tuple-element.87), kind=kOutput, calls=%fused_computation.41 | convolution fusion | flops 603979776 | bytes 3538944 | tf_op jit(solution)/shard_map/dot_general | solution.py:604
  61.6 2.2 %fusion.39.down_ref = f32[768,768]{1,0:T(8,128)} fusion(bf16[512,768]{1,0:T(8,128)(2,1)S(1)} %get-tuple-element.84, bf16[512,768]{1,0:T(8,128)(2,1)S(1)} %bitcast.89), kind=kOutput, calls=%fused_computation.104 | convolution fusion | flops 603979776 | bytes 3932160 | tf_op jit(solution)/shard_map/dot_general | solution.py:599
  63.9 0.8 fusion.1
  64.7 0.7 exponential_reduce_fusion
  65.7 1.0 multiply_reduce_fusion.3
  66.7 1.1 fusion.38.proj_ref
  67.8 1.0 fusion.28
  68.8 1.3 multiply_convert_fusion
  70.1 0.6 convolution_bitcast_fusion
  70.7 0.4 convolution_bitcast_fusion.1
  71.1 0.4 copy-done.26
  71.7 1.1 slice-done
  72.9 3.4 %fusion.32 = (f32[768]{0:T(1024)}, f32[768]{0:T(1024)}, bf16[512,768]{1,0:T(8,128)(2,1)}, f32[768]{0:T(1024)}, f32[768]{0:T(1024)}, /*index=5*/bf16[512,768]{1,0:T(8,128)(2,1)}, bf16[512,768]{1,0:T(8,128)(2,1)}) fusion(f32[512]{0:T(512)S(1)} %copy-done.39, f32[512]{0:T(512)S(1)} %copy-done.38, bf16[4,128,768]{2,1,0:T(8,128)(2,1)S(1)} %get-tuple-element.26, ...), kind=kOutput, calls=%fused_computation.97 | convolution fusion | flops 462222336 | bytes 6811648 | tf_op jit(solution)/shard_map/dot_general | solution.py:630
  76.3 0.8 reshape.308
  77.1 0.8 reshape.307
  77.9 0.8 reshape.309
  78.7 0.8 reshape.310
  79.4 1.2 fusion.8
  81.0 0.8 concatenate.57
  81.8 0.6 broadcast_in_dim.28.vec_ref
  82.4 3.3 %fusion.26.qkv_ref = f32[768,576]{1,0:T(8,128)} fusion(bf16[512,768]{1,0:T(8,128)(2,1)} %get-tuple-element.48, f32[512,192]{0,1:T(8,128)S(1)} %bitcast.101, f32[512,192]{0,1:T(8,128)S(1)} %bitcast.98, f32[512,192]{0,1:T(8,128)S(1)} %bitcast.95), kind=kOutput, calls=%fused_computation.94 | convolution fusion | flops 454754304 | bytes 3735552 | tf_op jit(solution)/shard_map/dot_general | solution.py:628
  85.8 0.4 fusion.40
  86.2 0.8 add_convert_fusion.1
  87.0 0.3 copy-done.16
  87.3 1.2 pad_maximum_fusion.parts_ref
  88.8 0.5 copy-done.17
  89.3 2.2 %fusion.12.up_ref = f32[768,768]{1,0:T(8,128)} fusion(bf16[512,768]{1,0:T(8,128)(2,1)S(1)} %copy-done.5, bf16[512,768]{1,0:T(8,128)(2,1)S(1)} %copy-done.17), kind=kOutput, calls=%fused_computation.43 | convolution fusion | flops 603979776 | bytes 3932160 | tf_op jit(solution)/shard_map/dot_general | solution.py:602
  91.5 72.8 %shard_map.246 = (bf16[128,768]{1,0:T(8,128)(2,1)}, f32[128,768]{1,0:T(8,128)}, f32[192,2304]{1,0:T(8,128)}, f32[192,768]{1,0:T(8,128)}, f32[192,3072]{1,0:T(8,1...) custom-call(f32[768,576]{1,0:T(8,128)} %fusion.26.qkv_ref, f32[768,768]{1,0:T(8,128)} %fusion.12.up_ref, ...), custom_call_target="tpu_custom_call" | custom-call | tf_op jit(solution)/shard_map/pallas_call | solution.py:663
  164.3 1.4 slice_reduce_fusion
  165.6 1.3 slice_reduce_fusion.1
  166.9 1.4 fusion.36
  168.3 0.6 copy.65
  168.9 1.6 copy.66
  170.5 1.8 copy.67
  172.3 2.9 %copy.68 = f32[192,2304]{1,0:T(8,128)} copy(f32[192,2304]{1,0:T(8,128)} %get-tuple-element.138) | data formatting | bytes 3538944
  175.2 0.8 copy.69
  176.0 1.4 copy.70
  177.4 1.1 copy-done.3
  178.6 1.4 copy.71
  (114 shorter events, 3.0 us)
Async XLA Ops:
  0.6 55.1 %copy-start = (bf16[768,768]{1,0:T(8,128)(2,1)S(1)}, bf16[768,768]{1,0:T(8,128)(2,1)}, u32[]{:S(2)}) copy-start(bf16[768,768]{1,0:T(8,128)(2,1)} %param.21) | copy-start | bytes 3538948
  0.7 10.6 %copy-start.1 = (bf16[128,768]{1,0:T(8,128)(2,1)S(1)}, bf16[128,768]{1,0:T(8,128)(2,1)}, u32[]{:S(2)}) copy-start(bf16[128,768]{1,0:T(8,128)(2,1)} %c_ref.3) | copy-start | bytes 589828
  0.7 10.6 %copy-start.2 = (bf16[128,768]{1,0:T(8,128)(2,1)S(1)}, bf16[128,768]{1,0:T(8,128)(2,1)}, u32[]{:S(2)}) copy-start(bf16[128,768]{1,0:T(8,128)(2,1)} %x_ref.3) | copy-start | bytes 589828
  8.2 46.0 %copy-start.23 = (f32[512,16]{0,1:T(8,128)}, f32[512,16]{0,1:T(8,128)S(1)}, u32[]{:S(2)}) copy-start(f32[512,16]{0,1:T(8,128)S(1)} %get-tuple-element.88) | copy-start | bytes 98308
  8.2 46.0 %copy-start.25 = (f32[512,16]{0,1:T(8,128)}, f32[512,16]{0,1:T(8,128)S(1)}, u32[]{:S(2)}) copy-start(f32[512,16]{0,1:T(8,128)S(1)} %get-tuple-element.89) | copy-start | bytes 98308
  44.2 4.1 %copy-start.11 = (bf16[192,768]{1,0:T(8,128)(2,1)S(1)}, bf16[192,768]{1,0:T(8,128)(2,1)}, u32[]{:S(2)}) copy-start(bf16[192,768]{1,0:T(8,128)(2,1)} %param.17) | copy-start | bytes 884740
  48.2 1.6 copy-start.31
  48.3 1.5 copy-start.33
  48.4 1.4 copy-start.35
  48.4 1.3 copy-start.10
  49.7 5.2 %copy-start.9 = (bf16[4,2,2,2,24,768]{5,4,3,2,1,0:T(8,128)(2,1)}, bf16[4,2,2,2,24,768]{5,4,3,2,1,0:T(8,128)(2,1)S(1)}, u32[]{:S(2)}) copy-start(bf16[4,2,2,2,24,768]{5,4,3,2,1,0:T(8,128)(2,1)S(1)} %copy.42) | copy-start | bytes 3538948
  49.7 1.6 copy-start.14
  61.6 2.3 %copy-start.13 = (pred[512,512]{0,1:T(8,128)(4,1)S(1)}, pred[512,512]{0,1:T(8,128)(4,1)}, u32[]{:S(2)}) copy-start(pred[512,512]{0,1:T(8,128)(4,1)} %iota_compare_fusion) | copy-start | bytes 786436
  61.6 2.3 %copy-start.20 = (bf16[512,3,48]{0,2,1:T(8,128)(2,1)S(1)}, bf16[512,3,48]{0,2,1:T(8,128)(2,1)}, u32[]{:S(2)}) copy-start(bf16[512,3,48]{0,2,1:T(8,128)(2,1)} %slice.175) | copy-start | bytes 442372
  61.6 2.3 %copy-start.21 = (bf16[512,3,48]{0,2,1:T(8,128)(2,1)S(1)}, bf16[512,3,48]{0,2,1:T(8,128)(2,1)}, u32[]{:S(2)}) copy-start(bf16[512,3,48]{0,2,1:T(8,128)(2,1)} %slice.174) | copy-start | bytes 442372
  61.6 2.2 %copy-start.29 = (bf16[512,3,16]{0,2,1:T(8,128)(2,1)S(1)}, bf16[512,3,16]{0,2,1:T(8,128)(2,1)}, u32[]{:S(2)}) copy-start(bf16[512,3,16]{0,2,1:T(8,128)(2,1)} %get-tuple-element.59) | copy-start | bytes 147460
  61.6 2.2 %copy-start.30 = (bf16[512,3,16]{0,2,1:T(8,128)(2,1)S(1)}, bf16[512,3,16]{0,2,1:T(8,128)(2,1)}, u32[]{:S(2)}) copy-start(bf16[512,3,16]{0,2,1:T(8,128)(2,1)} %get-tuple-element.60) | copy-start | bytes 147460
  64.6 0.9 copy-start.27
  64.7 1.0 copy-start.28
  66.7 1.2 copy-start.18
  68.8 4.1 %copy-start.7 = (f32[3,64,512]{2,1,0:T(8,128)}, f32[3,64,512]{2,1,0:T(8,128)S(1)}, u32[]{:S(2)}) copy-start(f32[3,64,512]{2,1,0:T(8,128)S(1)} %fusion.28) | copy-start | bytes 1179652
  70.7 0.9 copy-start.6
  70.7 0.8 copy-start.26
  70.7 0.8 copy-start.24
  71.5 1.4 copy-start.15
  71.5 1.4 copy-start.32
  71.5 1.4 copy-start.34
  71.6 1.4 copy-start.36
  71.6 1.4 copy-start.38
  71.6 1.4 copy-start.39
  71.6 1.2 slice-start
  76.3 6.1 %copy-start.8 = (f32[3,64,512]{2,1,0:T(8,128)S(1)}, f32[3,64,512]{2,1,0:T(8,128)}, u32[]{:S(2)}) copy-start(f32[3,64,512]{2,1,0:T(8,128)} %copy-done.7) | copy-start | bytes 1179652
  82.4 3.4 %copy-start.12 = (bf16[192,768]{1,0:T(8,128)(2,1)S(1)}, bf16[192,768]{1,0:T(8,128)(2,1)}, u32[]{:S(2)}) copy-start(bf16[192,768]{1,0:T(8,128)(2,1)} %param.17) | copy-start | bytes 884740
  82.4 3.4 %copy-start.19 = (bf16[3,64,512]{2,1,0:T(8,128)(2,1)S(1)}, bf16[3,64,512]{2,1,0:T(8,128)(2,1)}, u32[]{:S(2)}) copy-start(bf16[3,64,512]{2,1,0:T(8,128)(2,1)} %copy-done.18) | copy-start | bytes 589828
  86.2 1.1 copy-start.16
  87.3 1.4 copy-start.5
  87.3 1.9 %copy-start.17 = (bf16[512,768]{1,0:T(8,128)(2,1)S(1)}, bf16[512,768]{1,0:T(8,128)(2,1)}, u32[]{:S(2)}) copy-start(bf16[512,768]{1,0:T(8,128)(2,1)} %get-tuple-element.87) | copy-start | bytes 2359300
  168.3 6.9 %copy-start.37 = (f32[1,192]{1,0:T(1,128)}, f32[1,192]{1,0:T(1,128)S(1)}, u32[]{:S(2)}) copy-start(f32[1,192]{1,0:T(1,128)S(1)} %get-tuple-element.73) | copy-start | bytes 2308
  172.3 3.0 %copy-start.22 = (f32[192,768]{1,0:T(8,128)S(1)}, f32[192,768]{1,0:T(8,128)}, u32[]{:S(2)}) copy-start(f32[192,768]{1,0:T(8,128)} %get-tuple-element.140) | copy-start | bytes 1769476
  172.3 3.8 %copy-start.4 = (f32[192,3072]{1,0:T(8,128)S(1)}, f32[192,3072]{1,0:T(8,128)}, u32[]{:S(2)}) copy-start(f32[192,3072]{1,0:T(8,128)} %get-tuple-element.142) | copy-start | bytes 7077892
  176.0 2.5 %copy-start.3 = (f32[768,768]{1,0:T(8,128)S(1)}, f32[768,768]{1,0:T(8,128)}, u32[]{:S(2)}) copy-start(f32[768,768]{1,0:T(8,128)} %get-tuple-element.144) | copy-start | bytes 7077892

commit v3 on v2

--- a/solution.py
+++ b/solution.py
@@ -220,10 +220,10 @@
 
 def reduce_kernel(
     group, reps, rep_bits,
-    qkv_ref, up_ref, proj_ref, down_ref, vec_ref, parts_ref, x_ref, c_ref, bias_ref,
-    y_ref, dx_ref, qkv_out, proj_out, up_out, down_out, vec_out,
+    qkv_ref, up_ref, proj_ref, down_ref, sum_refs, parts_ref,
+    full_a, full_b, sr, vec_out, qkvb_out,
     buf_a, buf_b, r0_a, r0_b, r1_a, r1_b, r2_a, r2_b, up_send_a, up_send_b, ru_a, ru_b,
-    zr_a, zr_b, full_a, full_b, vs, vr, vz, sr,
+    zr_a, zr_b, vs, vr, vz,
     rs_send, rs_recv, u_send, u_recv, z_send, z_recv, g_send, g_recv,
     v_send, v_recv, vz_send, vz_recv, s_send, s_recv,
 ):
@@ -232,7 +232,7 @@
     r = lax.axis_index("rep")
     greet(group, reps, z, r, rep_bits)
     core = rep_bit(r, 0)
-    rows = x_ref.shape[0]
+    rows = parts_ref.shape[1] // 2
     own, width = proj_ref.shape
     unit = own // SPLIT
     hidden = up_ref.shape[1]
@@ -250,10 +250,19 @@
     zw = (zr_a.shape[-1], zr_b.shape[-1])
 
     sums = []
-    for t in range(1, group):
-        to = (z + t) % group
-        copy = remote(parts_ref.at[to], sr.at[t - 1], s_send.at[t], s_recv.at[t], {"cp": to})
-        sums.append(copy)
+    for i in range(2):
+        for t in range(1, group):
+            to = (z + t) % group
+            at = pl.ds(i * rows, rows)
+            sums.append(
+                remote(
+                    parts_ref.at[to, at],
+                    sr.at[t - 1, at],
+                    s_send.at[i, t],
+                    s_recv.at[i, t],
+                    {"cp": to},
+                )
+            )
 
     def fill(s, core_bit):
         first, second = s // 2, s % 2
@@ -294,14 +303,16 @@
             vs.at[k], vr.at[k], v_send.at[k], v_recv.at[k], {"rep": rep_partner(r, k)}
         )
 
+    for copy in sums[: group - 1]:
+        copy.start()
     fill_loop(1 - core)
     rs = [[rs_copy(h, s) for h in range(2)] for s in range(BITS)]
     for copy in rs[0]:
         copy.start()
-    vs[0] = vec_ref[...]
+    vs[0] = jnp.zeros(vs.shape[1:], f32)
+    for i, ref in enumerate(sum_refs):
+        vs[0, i : i + 1, : ref.shape[1]] = ref[...]
     v_copy(0).start()
-    for copy in sums:
-        copy.start()
     fill_loop(core)
 
     for h in range(2):
@@ -381,10 +392,12 @@
             )
         exchange.append(
             remote(
-                vs.at[rep_bits, to], vz.at[t - 1], vz_send.at[t], vz_recv.at[t], {"cp": to}
+                vs.at[rep_bits], vz.at[t - 1], vz_send.at[t], vz_recv.at[t], {"cp": to}
             )
         )
     for copy in exchange:
+        copy.start()
+    for copy in sums[group - 1 :]:
         copy.start()
 
     def mine_of(h):
@@ -401,11 +414,6 @@
         piece[z, :, : used[h]] = final[h][z, :, : used[h]]
         for t in range(1, group):
             piece[(z + group - t) % group, :, : used[h]] = zr[h][t - 1][:, : used[h]]
-    total = vs[rep_bits, z]
-    for t in range(1, group):
-        total = total + vz[t - 1]
-    vec_out[...] = total
-
     def g_copy(h, stage):
         d1, d2 = HALF_BITS[h]
         if stage == 0:
@@ -421,8 +429,37 @@
     gather = [[g_copy(h, s) for h in range(2)] for s in range(BITS)]
     for copy in gather[0]:
         copy.start()
+    total = vs[rep_bits]
+    qkvb_out[pl.ds(z, 1), :] = total[6:7, :qkv_cols]
+    shared = total[:5]
+    for t in range(1, group):
+        shared = shared + vz[t - 1, :5]
+        qkvb_out[pl.ds((z + group - t) % group, 1), :] = vz[t - 1, 6:7, :qkv_cols]
+    vec_out[...] = total
+    vec_out[:5] = shared
+    for s in range(BITS):
+        for h in range(2):
+            gather[s][h].wait()
+            if s + 1 < BITS:
+                gather[s + 1][h].start()
+
     for copy in sums:
         copy.wait()
+
+
+def finish_kernel(
+    group,
+    full_a, full_b, sr, parts_ref, x_ref, c_ref, bias_ref,
+    y_ref, dx_ref, qkv_out, proj_out, up_out, down_out,
+):
+    f32, bf16 = jnp.float32, jnp.bfloat16
+    z = lax.axis_index("cp")
+    rows = x_ref.shape[0]
+    own, width = proj_out.shape
+    unit = own // SPLIT
+    hidden = up_out.shape[1] // group
+    qkv_cols = qkv_out.shape[1] // group
+    cut = full_a.shape[-1] - hidden
     xs = x_ref[...].astype(f32)
     branch = xs + bias_ref[...]
     scaled = parts_ref[z, rows:].astype(f32)
@@ -439,12 +476,6 @@
         - jnp.mean(scaled, axis=-1, keepdims=True)
         - normed * jnp.mean(scaled * normed, axis=-1, keepdims=True)
     )
-    for s in range(BITS):
-        for h in range(2):
-            gather[s][h].wait()
-            if s + 1 < BITS:
-                gather[s + 1][h].start()
-
     def write(s, carry):
         c0, first, second = s // 4, (s // 2) % 2, s % 2
         base = s * unit
@@ -498,9 +529,15 @@
     score_scale = HEAD ** (-0.5)
 
     small = jnp.concatenate(
-        [qkv_bias, proj_bias, down_bias, attention_gain, attention_shift, feed_gain, feed_shift]
-    )
-    small = jnp.pad(small, (0, -small.shape[0] % 128))[None]
+        [qkv_bias.astype(f32).reshape(3, own)]
+        + [
+            vector.astype(f32)[None]
+            for vector in (
+                proj_bias, down_bias, attention_gain, attention_shift, feed_gain, feed_shift
+            )
+        ],
+        axis=0,
+    )
     unit = own // SPLIT
     r = lax.axis_index("rep")
     slot = rep_bit(r, 0) * 4 + rep_bit(r, 1) * 2 + rep_bit(r, 2)
@@ -522,7 +559,7 @@
         out_shape=[
             jax.ShapeDtypeStruct((group, rows, width), bf16),
             jax.ShapeDtypeStruct((group, rows, width), bf16),
-            jax.ShapeDtypeStruct((group,) + small.shape, bf16),
+            jax.ShapeDtypeStruct((group,) + small.shape, f32),
             jax.ShapeDtypeStruct((2, 2, 2) + up_piece.shape, bf16),
             jax.ShapeDtypeStruct((2, 2, 2) + qkv_piece.shape, bf16),
         ],
@@ -545,14 +582,11 @@
     )(block_input, out_cotangent, small, up_piece, qkv_piece)
     tokens = tokens.reshape(total_rows, width)
     cotangent = cotangent.reshape(total_rows, width)
-    small_all = small_all.reshape(group, -1)
-    joined_offset_all = small_all[:, :qkv_cols].reshape(group * qkv_cols)
     joined_offset = lax.dynamic_slice_in_dim(
-        joined_offset_all.reshape(3, group, own), rank, 1, axis=1
+        small_all[:, :3].reshape(3, group, own), rank, 1, axis=1
     ).reshape(qkv_cols)
     proj_offset, down_offset, gain_one, shift_one, gain_two, shift_two = (
-        small_all[:, qkv_cols + i * own : qkv_cols + (i + 1) * own].reshape(width)
-        for i in range(6)
+        small_all[:, 3 + i].reshape(width) for i in range(6)
     )
 
     up_matrix = up_slices.transpose(3, 0, 1, 2, 4, 5).reshape(width, hidden)
@@ -595,12 +629,12 @@
         activated, down_weight, preferred_element_type=f32
     )
 
-    bias_sum = jnp.sum(out_cotangent.astype(f32), axis=0)
+    bias_sum = jnp.sum(out_cotangent.astype(f32), axis=0, keepdims=True)
     down_grad = jnp.dot(activated.T, cotangent, preferred_element_type=f32)
     pre_grad = jnp.dot(cotangent, down_weight.T, preferred_element_type=f32) * gelu_slope(pre_act)
     pre_low = pre_grad.astype(bf16)
     up_grad = jnp.dot(feed_in.T, pre_low, preferred_element_type=f32)
-    up_bgrad = jnp.sum(pre_grad, axis=0)
+    up_bgrad = jnp.sum(pre_grad, axis=0, keepdims=True)
     feed_in_grad = jnp.dot(pre_low, up_matrix.T, preferred_element_type=f32)
     proj_grad = jnp.dot(context.T, cotangent, preferred_element_type=f32)
     context_grad = (
@@ -626,7 +660,7 @@
     )
     joined_low = joined_grad.astype(bf16)
     qkv_grad = jnp.dot(attn_in.T, joined_low, preferred_element_type=f32)
-    qkv_bgrad = jnp.sum(joined_grad, axis=0)
+    qkv_bgrad = jnp.sum(joined_grad, axis=0, keepdims=True)
     attn_in_grad = jnp.dot(joined_low, joined_matrix.T, preferred_element_type=f32)
 
     scaled_part = attn_in_grad * gain_one.astype(f32) + feed_in_grad * gain_two.astype(f32)
@@ -635,44 +669,33 @@
     ).astype(bf16)
     bias_row = (proj_offset.astype(f32) + down_offset.astype(f32))[None]
 
-    qkv_bgrad_placed = lax.dynamic_update_slice_in_dim(
-        jnp.zeros((3, group, own), f32), qkv_bgrad.reshape(3, 1, own), rank, axis=1
-    ).reshape(group, qkv_cols)
-    up_bgrad_placed = lax.dynamic_update_slice_in_dim(
-        jnp.zeros((group, hidden), f32), up_bgrad[None], rank, axis=0
-    )
-    vectors = jnp.concatenate(
-        [qkv_bgrad_placed, up_bgrad_placed]
-        + [
-            term.reshape(group, own)
-            for term in (
-                bias_sum,
-                jnp.sum(attn_in_grad * normed, axis=0),
-                jnp.sum(attn_in_grad, axis=0),
-                jnp.sum(feed_in_grad * normed, axis=0),
-                jnp.sum(feed_in_grad, axis=0),
-            )
-        ],
-        axis=1,
-    )
+    row_sums = [
+        bias_sum,
+        jnp.sum(attn_in_grad * normed, axis=0, keepdims=True),
+        jnp.sum(attn_in_grad, axis=0, keepdims=True),
+        jnp.sum(feed_in_grad * normed, axis=0, keepdims=True),
+        jnp.sum(feed_in_grad, axis=0, keepdims=True),
+        up_bgrad,
+        qkv_bgrad,
+    ]
+    table = (8, max(width, hidden, qkv_cols))
+
     rep_bits = reps.bit_length() - 1
     half_w = (qkv_cols + own + width + hidden) // 2
     piece = (group, unit, half_w)
     halves = lambda *lead: [pltpu.VMEM(lead + piece, bf16)] * 2
     spare = max(rep_bits - BITS, 1)
-    (block_output, input_grad, qkv_out, proj_out, up_out, down_out, vectors) = pl.pallas_call(
+    slices_a, slices_b, received, vectors, qkvb_all = pl.pallas_call(
         functools.partial(reduce_kernel, group, reps, rep_bits),
         out_shape=[
-            jax.ShapeDtypeStruct((rows, width), bf16),
-            jax.ShapeDtypeStruct((rows, width), f32),
-            jax.ShapeDtypeStruct((own, group * qkv_cols), f32),
-            jax.ShapeDtypeStruct((own, width), f32),
-            jax.ShapeDtypeStruct((own, group * hidden), f32),
-            jax.ShapeDtypeStruct((hidden, width), f32),
-            jax.ShapeDtypeStruct((1, vectors.shape[1]), f32),
+            jax.ShapeDtypeStruct((2, 2, 2) + piece, bf16),
+            jax.ShapeDtypeStruct((2, 2, 2) + piece, bf16),
+            jax.ShapeDtypeStruct((group - 1, 2 * rows, width), bf16),
+            jax.ShapeDtypeStruct(table, f32),
+            jax.ShapeDtypeStruct((group, qkv_cols), f32),
         ],
-        in_specs=[vmem] * 9,
-        out_specs=[vmem] * 7,
+        in_specs=[vmem] * 4 + [[vmem] * 7] + [vmem],
+        out_specs=[vmem] * 5,
         scratch_shapes=(
             halves(2, 2, 2)
             + halves(2, 2)
@@ -684,12 +707,10 @@
                 pltpu.VMEM((group - 1, unit, hidden), bf16),
                 pltpu.VMEM((group - 1, unit, -(-qkv_cols // 128) * 128), bf16),
             ]
-            + halves(2, 2, 2)
             + [
-                pltpu.VMEM((rep_bits + 1, group, 1, vectors.shape[1]), f32),
-                pltpu.VMEM((rep_bits, group, 1, vectors.shape[1]), f32),
-                pltpu.VMEM((group - 1, 1, vectors.shape[1]), f32),
-                pltpu.VMEM((group - 1, 2 * rows, width), bf16),
+                pltpu.VMEM((rep_bits + 1,) + table, f32),
+                pltpu.VMEM((rep_bits,) + table, f32),
+                pltpu.VMEM((group - 1,) + table, f32),
                 dma((2, BITS)),
                 dma((2, BITS)),
                 dma((2, spare)),
@@ -702,8 +723,8 @@
                 dma((rep_bits,)),
                 dma((group,)),
                 dma((group,)),
-                dma((group,)),
-                dma((group,)),
+                dma((2, group)),
+                dma((2, group)),
             ]
         ),
         compiler_params=pltpu.CompilerParams(
@@ -714,20 +735,29 @@
         up_grad,
         proj_grad,
         down_grad,
-        vectors[:, None],
+        row_sums,
         parts,
-        block_input,
-        out_cotangent,
-        bias_row,
-    )
-    vectors = vectors[0]
-    cuts = [qkv_cols, qkv_cols + hidden] + [
-        qkv_cols + hidden + i * own for i in range(1, 5)
-    ]
-    (qkvb_out, upb_out, bias_out, gain1_out, shift1_out, gain2_out, shift2_out) = jnp.split(
-        vectors, cuts
-    )
-
+    )
+    block_output, input_grad, qkv_out, proj_out, up_out, down_out = pl.pallas_call(
+        functools.partial(finish_kernel, group),
+        out_shape=[
+            jax.ShapeDtypeStruct((rows, width), bf16),
+            jax.ShapeDtypeStruct((rows, width), f32),
+            jax.ShapeDtypeStruct((own, group * qkv_cols), f32),
+            jax.ShapeDtypeStruct((own, width), f32),
+            jax.ShapeDtypeStruct((own, group * hidden), f32),
+            jax.ShapeDtypeStruct((hidden, width), f32),
+        ],
+        in_specs=[vmem] * 7,
+        out_specs=[vmem] * 6,
+        compiler_params=pltpu.CompilerParams(vmem_limit_bytes=40 * 2**20),
+    )(slices_a, slices_b, received, parts, block_input, out_cotangent, bias_row)
+    owned = lax.dynamic_slice_in_dim(vectors[:5, :width], rank * own, own, axis=1)
+    bias_out, gain1_out, shift1_out, gain2_out, shift2_out = (owned[i] for i in range(5))
+    upb_out = vectors[5, :hidden]
+    qkvb_out = lax.dynamic_slice_in_dim(
+        qkvb_all.reshape(group, 3, own).transpose(1, 0, 2).reshape(-1), rank * qkv_cols, qkv_cols
+    )
     return (
         block_output,
         input_grad,

time: 183 us -> 156 us (0.85); the launches traced: 180 us -> 156 us
  local copies, waits for them, and re-layouts: 38.6 us -> 19.7 us
  matrix products: 25.4 us -> 21.2 us
  other arithmetic: 8.94 us -> 4.89 us
  Pallas kernels: 106 us -> 109 us
    unnamed x88 -> x47, local copies, waits for them, and re-layouts: 14.7 us -> 7.48 us
    concatenate x2 -> x1, local copies, waits for them, and re-layouts: 5.66 us -> 0.04 us  [body(): jnp.concatenate([qkv_bias.astype(f32).reshape(3, own)] + [vector.astype(f...]
    pallas_call x0 -> x1, Pallas kernels: none -> 4.55 us  [body(): pl.pallas_call(functools.partial(finish_kernel, group), out_shape=[jax.Sh...]
    split x3 -> x0, local copies, waits for them, and re-layouts: 4.03 us -> none  [body(): jnp.split(vectors, cuts)]
    reshape x7 -> x4, local copies, waits for them, and re-layouts: 3.92 us -> 0.27 us  [the longest x2 0.17 us: body(): qkvb_all.reshape(group, 3, own).transpose(1, 0, 2).reshape(-1)]
    slice x1 -> x3, local copies, waits for them, and re-layouts: 0.01 us -> 2.88 us  [the longest x1 1.54 us: body(): owned[i]]
    broadcast_in_dim x5 -> x13, local copies, waits for them, and re-layouts: 1.24 us -> 4.11 us  [the longest x1 0.59 us: body(): jnp.sum(feed_in_grad, axis=0, keepdims=True)]
    pallas_call x1, Pallas kernels: 72.8 us -> 70.7 us  [body(): pl.pallas_call(functools.partial(reduce_kernel, group, reps, rep_bits), o...]
where the time goes in v3:
time: 156 us
  Pallas kernels  109 us (70%)
  matrix products  21.2 us (14%)
  local copies, waits for them, and re-layouts  19.7 us (13%)
  other arithmetic  4.89 us (3%)
    pallas_call x1, Pallas kernels, body(): pl.pallas_call(functools.partial(reduce_kernel, group, reps, rep_bits), o...  70.7 us
    pallas_call x1, Pallas kernels, body(): pl.pallas_call(functools.partial(gather_kernel, group, reps), out_shape=[...  33.5 us
    unnamed x47, local copies, waits for them, and re-layouts  7.48 us
    pallas_call x1, Pallas kernels, body(): pl.pallas_call(functools.partial(finish_kernel, group), out_shape=[jax.Sh...  4.55 us

profile of v3, /device:TPU:11, one launch (start us, length us, event | category | flops | bytes accessed | tf_op | source)
XLA Modules:
  0.0 155.8 jit_solution(9872412411923490159)
XLA Ops:
  0.8 1.1 constant_dynamic-slice_fusion.1
  2.0 0.2 reshape.229
  2.1 0.1 copy.35
  2.2 0.2 reshape.230.pq_ref
  2.4 0.9 constant_dynamic-slice_fusion.2
  3.3 0.1 reshape.227
  3.6 33.5 %shard_map.245 = (bf16[4,128,768]{2,1,0:T(8,128)(2,1)S(1)}, bf16[4,128,768]{2,1,0:T(8,128)(2,1)S(1)}, f32[4,9,192]{2,1,0:T(8,128)S(1)}, bf16[2,2,2,4,24,768]{5,4...) custom-call(bf16[128,768]{1,0:T(8,128)(2,1)S(1)} %copy-done.8, bf16[128,768]{1,0:T(8,128)(2,1)S(1)} %copy-done.4, ...), custom_call_target="tpu_custom_call" | custom-call | tf_op jit(solution)/shard_map/pallas_call | solution.py:557
  37.1 0.9 copy-done.6
  38.1 0.1 add.147
  38.2 0.1 add.161
  38.3 0.1 mul.230
  38.3 0.1 mul.255
  38.4 0.2 convert_reduce_fusion
  38.6 0.4 multiply_reduce_fusion.2
  39.0 1.6 %add_convert_fusion.2 = (bf16[4,128,768]{2,1,0:T(8,128)(2,1)}, bf16[4,128,768]{2,1,0:T(8,128)(2,1)}) fusion(bf16[4,128,768]{2,1,0:T(8,128)(2,1)S(1)} %get-tuple-element.30, f32[768]{0:T(1024)S(1)} %add.161, f32[768]{0:T(1024)S(1)} %mul.255, f32[4,128]{1,0:T(4,128)S(1)} %get-tuple-element.85, f32[4,128]{1,0:T(4,128)S(1)} %get-tuple-element.88, ...), kind=kLoop, calls=%fused_computation.21 | loop fusion | flops 3538944 | bytes 2375680 | tf_op jit(solution)/shard_map/convert_element_type | solution.py:602
  40.6 1.0 copy.36
  41.7 0.1 add.153
  41.8 2.1 %convolution_add_fusion.1 = f32[512,576]{0,1:T(8,128)S(1)} fusion(bf16[512,768]{1,0:T(8,128)(2,1)} %bitcast.114, bf16[768,576]{1,0:T(8,128)(2,1)} %bitcast.110, f32[576]{0:T(1024)S(1)} %add.153), kind=kOutput, calls=%fused_computation.27 | convolution fusion | flops 453279744 | bytes 2853120 | tf_op jit(solution)/shard_map/dot_general | solution.py:604
  44.0 0.1 multiply_cosine_fusion
  44.3 0.1 iota_compare_fusion
  44.4 0.8 fusion.1
  45.1 0.7 exponential_reduce_fusion
  45.9 0.2 copy-done.10
  46.1 0.4 convolution_convert_fusion.1
  46.5 1.0 multiply_reduce_fusion.3
  47.5 0.4 fusion.40
  48.0 0.8 copy-done.9
  48.8 0.1 copy.42
  48.9 0.3 copy-done.12
  49.2 0.9 multiply_convert_fusion.1
  50.1 0.8 add_convert_fusion.1
  50.9 1.3 multiply_convert_fusion
  52.2 0.4 convolution_bitcast_fusion.1
  52.6 0.6 convolution_bitcast_fusion
  53.4 1.0 fusion.28
  54.4 1.1 fusion.37
  55.5 0.8 fusion.10
  56.3 0.4 copy-done.11
  56.7 2.0 %fusion.32 = (f32[768]{0:T(1024)S(1)}, f32[768]{0:T(1024)S(1)}, bf16[512,768]{1,0:T(8,128)(2,1)S(1)}, f32[768]{0:T(1024)S(1)}, f32[768]{0:T(1024)S(1)}, /*index=...) fusion(f32[512]{0:T(512)S(1)} %get-tuple-element.86, f32[512]{0:T(512)S(1)} %get-tuple-element.87, ...), kind=kOutput, calls=%fused_computation.96 | convolution fusion | flops 462222336 | bytes 6811648 | tf_op jit(solution)/shard_map/dot_general | solution.py:664
  58.7 1.2 pad_maximum_fusion.parts_ref
  59.9 0.2 fusion.8
  60.1 0.6 broadcast_in_dim.91.sum_refs_6_
  60.7 2.2 %fusion.12.up_ref = f32[768,768]{1,0:T(8,128)} fusion(bf16[512,768]{1,0:T(8,128)(2,1)S(1)} %get-tuple-element.60, bf16[512,768]{1,0:T(8,128)(2,1)S(1)} %get-tuple-element.96), kind=kOutput, calls=%fused_computation.43 | convolution fusion | flops 603979776 | bytes 3932160 | tf_op jit(solution)/shard_map/dot_general | solution.py:636
  62.9 2.1 %fusion.26.qkv_ref = f32[768,576]{1,0:T(8,128)} fusion(bf16[512,768]{1,0:T(8,128)(2,1)S(1)} %get-tuple-element.61, f32[512,192]{0,1:T(8,128)S(1)} %bitcast.100, f32[512,192]{0,1:T(8,128)S(1)} %bitcast.97, f32[512,192]{0,1:T(8,128)S(1)} %bitcast.94), kind=kOutput, calls=%fused_computation.93 | convolution fusion | flops 454754304 | bytes 3735552 | tf_op jit(solution)/shard_map/dot_general | solution.py:662
  65.0 0.6 broadcast_in_dim.86.sum_refs_1_
  65.6 0.6 broadcast_in_dim.87.sum_refs_2_
  66.1 0.6 broadcast_in_dim.88.sum_refs_3_
  66.7 0.6 broadcast_in_dim.89.sum_refs_4_
  67.3 1.1 fusion.38.proj_ref
  68.5 2.2 %fusion.39.down_ref = f32[768,768]{1,0:T(8,128)} fusion(bf16[512,768]{1,0:T(8,128)(2,1)S(1)} %get-tuple-element.93, bf16[512,768]{1,0:T(8,128)(2,1)S(1)} %bitcast.89), kind=kOutput, calls=%fused_computation.103 | convolution fusion | flops 603979776 | bytes 3932160 | tf_op jit(solution)/shard_map/dot_general | solution.py:633
  70.7 0.6 broadcast_in_dim.90.sum_refs_5_
  71.3 0.6 broadcast_in_dim.85.sum_refs_0_
  71.9 70.7 %shard_map.246 = (bf16[2,2,2,4,24,1152]{5,4,3,2,1,0:T(8,128)(2,1)}, bf16[2,2,2,4,24,1152]{5,4,3,2,1,0:T(8,128)(2,1)}, bf16[3,256,768]{2,1,0:T(8,128)(2,1)}, f32[8,768]{1,0:T(8,128)}, f32[4,576]{1,0:T(4,128)}) custom-call(f32[768,576]{1,0:T(8,128)} %fusion.26.qkv_ref, f32[768,768]{1,0:T(8,128)} %fusion.12.up_ref, f32[192,768]{1,0:T(8,128)} %fusion.38.proj_ref, ...), custom_call_target="tpu_custom_call" | custom-call | tf_op jit(solution)/shard_map/pallas_call | solution.py:688
  142.6 0.1 add.173.bias_ref
  142.7 1.5 copy-done.2
  144.2 1.5 copy-done.3
  145.7 1.3 copy-done.5
  147.0 4.6 %shard_map.247 = (bf16[128,768]{1,0:T(8,128)(2,1)}, f32[128,768]{1,0:T(8,128)}, f32[192,2304]{1,0:T(8,128)}, f32[192,768]{1,0:T(8,128)}, f32[192,3072]{1,0:T(8,128)}, /*index=5*/f32[768,768]{1,0:T(8,128)}) custom-call(bf16[2,2,2,4,24,1152]{5,4,3,2,1,0:T(8,128)(2,1)S(1)} %copy-done.2, bf16[2,2,2,4,24,1152]{5,4,3,2,1,0:T(8,128)(2,1)S(1)} %copy-done.3, ...), custom_call_target="tpu_custom_call" | custom-call | tf_op jit(solution)/shard_map/pallas_call | solution.py:741
  151.5 0.1 reshape.244
  151.6 0.1 reshape.245
  151.7 0.7 dynamic_slice.18
  152.4 1.5 fusion.36
  153.9 1.3 slice_reduce_fusion.4
  155.2 0.6 copy.55
  (74 shorter events, 0.8 us)
Async XLA Ops:
  0.7 49.4 %copy-start = (bf16[768,768]{1,0:T(8,128)(2,1)S(1)}, bf16[768,768]{1,0:T(8,128)(2,1)}, u32[]{:S(2)}) copy-start(bf16[768,768]{1,0:T(8,128)(2,1)} %param.21) | copy-start | bytes 3538948
  0.7 2.7 %copy-start.16 = (bf16[576]{0:T(1024)(128)(2,1)S(1)}, bf16[576]{0:T(1024)(128)(2,1)}, u32[]{:S(2)}) copy-start(bf16[576]{0:T(1024)(128)(2,1)} %param.16) | copy-start | bytes 3460
  0.7 2.8 %copy-start.17 = (bf16[192]{0:T(256)(128)(2,1)S(1)}, bf16[192]{0:T(256)(128)(2,1)}, u32[]{:S(2)}) copy-start(bf16[192]{0:T(256)(128)(2,1)} %param.18) | copy-start | bytes 1156
  0.7 2.8 %copy-start.18 = (bf16[192]{0:T(256)(128)(2,1)S(1)}, bf16[192]{0:T(256)(128)(2,1)}, u32[]{:S(2)}) copy-start(bf16[192]{0:T(256)(128)(2,1)} %param.22) | copy-start | bytes 1156
  0.7 2.8 %copy-start.19 = (bf16[192]{0:T(256)(128)(2,1)S(1)}, bf16[192]{0:T(256)(128)(2,1)}, u32[]{:S(2)}) copy-start(bf16[192]{0:T(256)(128)(2,1)} %param.23) | copy-start | bytes 1156
  0.7 2.8 %copy-start.20 = (bf16[192]{0:T(256)(128)(2,1)S(1)}, bf16[192]{0:T(256)(128)(2,1)}, u32[]{:S(2)}) copy-start(bf16[192]{0:T(256)(128)(2,1)} %param.24) | copy-start | bytes 1156
  0.7 2.8 %copy-start.21 = (bf16[192]{0:T(256)(128)(2,1)S(1)}, bf16[192]{0:T(256)(128)(2,1)}, u32[]{:S(2)}) copy-start(bf16[192]{0:T(256)(128)(2,1)} %param.25) | copy-start | bytes 1156
  0.7 2.8 %copy-start.22 = (bf16[192]{0:T(256)(128)(2,1)S(1)}, bf16[192]{0:T(256)(128)(2,1)}, u32[]{:S(2)}) copy-start(bf16[192]{0:T(256)(128)(2,1)} %param.26) | copy-start | bytes 1156
  0.7 2.9 %copy-start.8 = (bf16[128,768]{1,0:T(8,128)(2,1)S(1)}, bf16[128,768]{1,0:T(8,128)(2,1)}, u32[]{:S(2)}) copy-start(bf16[128,768]{1,0:T(8,128)(2,1)} %x_ref.3) | copy-start | bytes 589828
  0.7 2.9 %copy-start.4 = (bf16[128,768]{1,0:T(8,128)(2,1)S(1)}, bf16[128,768]{1,0:T(8,128)(2,1)}, u32[]{:S(2)}) copy-start(bf16[128,768]{1,0:T(8,128)(2,1)} %c_ref.3) | copy-start | bytes 589828
  37.1 0.9 copy-start.6
  38.6 2.0 %copy-start.7 = (bf16[2,2,2,4,24,576]{5,4,3,2,1,0:T(8,128)(2,1)S(1)}, bf16[2,2,2,4,24,576]{5,4,3,2,1,0:T(8,128)(2,1)}, u32[]{:S(2)}) copy-start(bf16[2,2,2,4,24,576]{5,4,3,2,1,0:T(8,128)(2,1)} %copy-done.6) | copy-start | bytes 2654212
  45.1 1.0 copy-start.10
  47.5 1.3 copy-start.9
  48.0 1.0 copy-start.15
  48.0 1.2 copy-start.12
  55.5 1.2 copy-start.11
  71.9 70.8 %copy-start.1 = (bf16[4,256,768]{2,1,0:T(8,128)(2,1)S(1)}, bf16[4,256,768]{2,1,0:T(8,128)(2,1)}, u32[]{:S(2)}) copy-start(bf16[4,256,768]{2,1,0:T(8,128)(2,1)} %pad_maximum_fusion.parts_ref) | copy-start | bytes 4718596
  142.7 1.5 copy-start.2
  144.2 1.5 copy-start.3
  145.7 1.3 copy-start.5
  146.9 4.6 %copy-start.13 = (f32[4,576]{1,0:T(4,128)S(1)}, f32[4,576]{1,0:T(4,128)}, u32[]{:S(2)}) copy-start(f32[4,576]{1,0:T(4,128)} %get-tuple-element.41) | copy-start | bytes 27652
  153.9 1.9 %copy-start.14 = (f32[1,192]{1,0:T(1,128)}, f32[1,192]{1,0:T(1,128)S(1)}, u32[]{:S(2)}) copy-start(f32[1,192]{1,0:T(1,128)S(1)} %get-tuple-element.82) | copy-start | bytes 2308

commit v4 on v3

--- a/solution.py
+++ b/solution.py
@@ -311,7 +311,7 @@
         copy.start()
     vs[0] = jnp.zeros(vs.shape[1:], f32)
     for i, ref in enumerate(sum_refs):
-        vs[0, i : i + 1, : ref.shape[1]] = ref[...]
+        vs[0, i, : ref.shape[0]] = ref[...]
     v_copy(0).start()
     fill_loop(core)
 
@@ -629,12 +629,12 @@
         activated, down_weight, preferred_element_type=f32
     )
 
-    bias_sum = jnp.sum(out_cotangent.astype(f32), axis=0, keepdims=True)
+    bias_sum = jnp.sum(out_cotangent.astype(f32), axis=0)
     down_grad = jnp.dot(activated.T, cotangent, preferred_element_type=f32)
     pre_grad = jnp.dot(cotangent, down_weight.T, preferred_element_type=f32) * gelu_slope(pre_act)
     pre_low = pre_grad.astype(bf16)
     up_grad = jnp.dot(feed_in.T, pre_low, preferred_element_type=f32)
-    up_bgrad = jnp.sum(pre_grad, axis=0, keepdims=True)
+    up_bgrad = jnp.sum(pre_grad, axis=0)
     feed_in_grad = jnp.dot(pre_low, up_matrix.T, preferred_element_type=f32)
     proj_grad = jnp.dot(context.T, cotangent, preferred_element_type=f32)
     context_grad = (
@@ -660,7 +660,7 @@
     )
     joined_low = joined_grad.astype(bf16)
     qkv_grad = jnp.dot(attn_in.T, joined_low, preferred_element_type=f32)
-    qkv_bgrad = jnp.sum(joined_grad, axis=0, keepdims=True)
+    qkv_bgrad = jnp.sum(joined_grad, axis=0)
     attn_in_grad = jnp.dot(joined_low, joined_matrix.T, preferred_element_type=f32)
 
     scaled_part = attn_in_grad * gain_one.astype(f32) + feed_in_grad * gain_two.astype(f32)
@@ -671,10 +671,10 @@
 
     row_sums = [
         bias_sum,
-        jnp.sum(attn_in_grad * normed, axis=0, keepdims=True),
-        jnp.sum(attn_in_grad, axis=0, keepdims=True),
-        jnp.sum(feed_in_grad * normed, axis=0, keepdims=True),
-        jnp.sum(feed_in_grad, axis=0, keepdims=True),
+        jnp.sum(attn_in_grad * normed, axis=0),
+        jnp.sum(attn_in_grad, axis=0),
+        jnp.sum(feed_in_grad * normed, axis=0),
+        jnp.sum(feed_in_grad, axis=0),
         up_bgrad,
         qkv_bgrad,
     ]

time: 156 us -> 155 us (level)
  local copies, waits for them, and re-layouts: 19.7 us -> 15.7 us
    broadcast_in_dim x7 -> x0, local copies, waits for them, and re-layouts: 4.09 us -> none  [the longest x1 0.59 us: body(): jnp.sum(feed_in_grad, axis=0, keepdims=True)]
where the time goes in v4:
time: 155 us; the launch traced here: 154 us
  Pallas kernels  109 us (70%)
  matrix products  22.4 us (14%)
  local copies, waits for them, and re-layouts  15.7 us (10%)
  other arithmetic  6.05 us (4%)
    pallas_call x1, Pallas kernels, body(): pl.pallas_call(functools.partial(reduce_kernel, group, reps, rep_bits), o...  70.7 us
    pallas_call x1, Pallas kernels, body(): pl.pallas_call(functools.partial(gather_kernel, group, reps), out_shape=[...  33.5 us
    unnamed x47, local copies, waits for them, and re-layouts  7.5 us
    pallas_call x1, Pallas kernels, body(): pl.pallas_call(functools.partial(finish_kernel, group), out_shape=[jax.Sh...  4.55 us

profile of v4, /device:TPU:11, one launch (start us, length us, event | category | flops | bytes accessed | tf_op | source)
XLA Modules:
  0.0 154.1 jit_solution(6592100368809717964)
XLA Ops:
  0.7 0.0 copy-start
  0.8 1.1 constant_dynamic-slice_fusion.1
  2.0 0.2 reshape.229
  2.1 0.1 copy.35
  2.2 0.2 reshape.230.pq_ref
  2.4 0.9 constant_dynamic-slice_fusion.2
  3.3 0.1 reshape.227
  3.6 33.5 %shard_map.245 = (bf16[4,128,768]{2,1,0:T(8,128)(2,1)S(1)}, bf16[4,128,768]{2,1,0:T(8,128)(2,1)S(1)}, f32[4,9,192]{2,1,0:T(8,128)S(1)}, bf16[2,2,2,4,24,768]{5,4...) custom-call(bf16[128,768]{1,0:T(8,128)(2,1)S(1)} %copy-done.8, bf16[128,768]{1,0:T(8,128)(2,1)S(1)} %copy-done.4, ...), custom_call_target="tpu_custom_call" | custom-call | tf_op jit(solution)/shard_map/pallas_call | solution.py:557
  37.1 0.0 copy-start.6
  37.1 0.9 copy-done.6
  38.0 0.1 add_reduce_fusion
  38.1 0.1 add.147
  38.2 0.1 add.161
  38.3 0.1 mul.230
  38.3 0.1 mul.255
  38.4 0.2 convert_reduce_fusion
  38.6 0.0 copy-start.7
  38.6 0.4 multiply_reduce_fusion.2
  39.0 1.6 %add_convert_fusion.2 = (bf16[4,128,768]{2,1,0:T(8,128)(2,1)}, bf16[4,128,768]{2,1,0:T(8,128)(2,1)}) fusion(bf16[4,128,768]{2,1,0:T(8,128)(2,1)S(1)} %get-tuple-element.30, f32[768]{0:T(1024)S(1)} %add.161, f32[768]{0:T(1024)S(1)} %mul.255, f32[4,128]{1,0:T(4,128)S(1)} %get-tuple-element.85, f32[4,128]{1,0:T(4,128)S(1)} %get-tuple-element.88, ...), kind=kLoop, calls=%fused_computation.21 | loop fusion | flops 3538944 | bytes 2375680 | tf_op jit(solution)/shard_map/convert_element_type | solution.py:602
  40.6 1.0 copy.36
  41.7 0.1 add.153
  41.8 2.1 %convolution_add_fusion.1 = f32[512,576]{0,1:T(8,128)S(1)} fusion(bf16[512,768]{1,0:T(8,128)(2,1)} %bitcast.114, bf16[768,576]{1,0:T(8,128)(2,1)} %bitcast.110, f32[576]{0:T(1024)S(1)} %add.153), kind=kOutput, calls=%fused_computation.27 | convolution fusion | flops 453279744 | bytes 2853120 | tf_op jit(solution)/shard_map/dot_general | solution.py:604
  43.9 0.1 fusion.33
  44.0 0.1 multiply_cosine_fusion
  44.3 0.1 iota_compare_fusion
  44.4 0.8 fusion.1
  45.1 0.7 exponential_reduce_fusion
  45.9 0.2 copy-done.10
  46.1 0.4 convolution_convert_fusion.1
  46.5 1.0 multiply_reduce_fusion.3
  47.5 0.4 fusion.40
  48.0 0.0 copy-start.12
  48.0 0.8 copy-done.9
  48.8 0.1 copy.42
  48.9 0.3 copy-done.12
  49.2 0.9 multiply_convert_fusion.1
  50.1 0.8 add_convert_fusion.1
  50.9 1.3 multiply_convert_fusion
  52.2 0.4 convolution_bitcast_fusion.1
  52.5 0.6 convolution_bitcast_fusion
  53.4 1.0 fusion.28
  54.4 1.7 %fusion.37 = (f32[768]{0:T(1024)}, bf16[512,768]{1,0:T(8,128)(2,1)S(1)}) fusion(f32[512,768]{1,0:T(8,128)S(1)} %get-tuple-element.94, bf16[512,768]{1,0:T(8,128)(2,1)S(1)} %bitcast.87, bf16[768,768]{1,0:T(8,128)(2,1)S(1)} %copy-done), kind=kOutput, calls=%fused_computation.101 | convolution fusion | flops 608304384 | bytes 4328448 | tf_op jit(solution)/shard_map/dot_general | solution.py:634
  56.1 0.8 fusion.10
  56.9 0.4 copy-done.11
  57.3 2.6 %fusion.32 = (f32[768]{0:T(1024)}, f32[768]{0:T(1024)}, bf16[512,768]{1,0:T(8,128)(2,1)S(1)}, f32[768]{0:T(1024)}, f32[768]{0:T(1024)}, /*index=5*/bf16[512,768]{1,0:T(8,128)(2,1)S(1)}, bf16[512,768]{1,0:T(8,128)(2,1)S(1)}) fusion(f32[512]{0:T(512)S(1)} %get-tuple-element.86, f32[512]{0:T(512)S(1)} %get-tuple-element.87, ...), kind=kOutput, calls=%fused_computation.96 | convolution fusion | flops 462222336 | bytes 6811648 | tf_op jit(solution)/shard_map/dot_general | solution.py:664
  59.8 1.2 pad_maximum_fusion.parts_ref
  61.1 0.8 fusion.8.sum_refs_6_
  61.8 2.2 %fusion.12.up_ref = f32[768,768]{1,0:T(8,128)} fusion(bf16[512,768]{1,0:T(8,128)(2,1)S(1)} %get-tuple-element.60, bf16[512,768]{1,0:T(8,128)(2,1)S(1)} %get-tuple-element.96), kind=kOutput, calls=%fused_computation.43 | convolution fusion | flops 603979776 | bytes 3932160 | tf_op jit(solution)/shard_map/dot_general | solution.py:636
  64.1 2.1 %fusion.26.qkv_ref = f32[768,576]{1,0:T(8,128)} fusion(bf16[512,768]{1,0:T(8,128)(2,1)S(1)} %get-tuple-element.61, f32[512,192]{0,1:T(8,128)S(1)} %bitcast.100, f32[512,192]{0,1:T(8,128)S(1)} %bitcast.97, f32[512,192]{0,1:T(8,128)S(1)} %bitcast.94), kind=kOutput, calls=%fused_computation.93 | convolution fusion | flops 454754304 | bytes 3735552 | tf_op jit(solution)/shard_map/dot_general | solution.py:662
  66.2 1.1 fusion.38.proj_ref
  67.3 2.2 %fusion.39.down_ref = f32[768,768]{1,0:T(8,128)} fusion(bf16[512,768]{1,0:T(8,128)(2,1)S(1)} %get-tuple-element.93, bf16[512,768]{1,0:T(8,128)(2,1)S(1)} %bitcast.89), kind=kOutput, calls=%fused_computation.103 | convolution fusion | flops 603979776 | bytes 3932160 | tf_op jit(solution)/shard_map/dot_general | solution.py:633
  69.5 0.6 convert_reduce_fusion.1.sum_refs_0_
  70.2 70.7 %shard_map.246 = (bf16[2,2,2,4,24,1152]{5,4,3,2,1,0:T(8,128)(2,1)}, bf16[2,2,2,4,24,1152]{5,4,3,2,1,0:T(8,128)(2,1)}, bf16[3,256,768]{2,1,0:T(8,128)(2,1)}, f32[8,768]{1,0:T(8,128)}, f32[4,576]{1,0:T(4,128)}) custom-call(f32[768,576]{1,0:T(8,128)} %fusion.26.qkv_ref, f32[768,768]{1,0:T(8,128)} %fusion.12.up_ref, f32[192,768]{1,0:T(8,128)} %fusion.38.proj_ref, ...), custom_call_target="tpu_custom_call" | custom-call | tf_op jit(solution)/shard_map/pallas_call | solution.py:688
  140.9 0.1 add.173.bias_ref
  141.0 1.5 copy-done.2
  142.5 1.5 copy-done.3
  143.9 1.3 copy-done.5
  145.2 4.6 %shard_map.247 = (bf16[128,768]{1,0:T(8,128)(2,1)}, f32[128,768]{1,0:T(8,128)}, f32[192,2304]{1,0:T(8,128)}, f32[192,768]{1,0:T(8,128)}, f32[192,3072]{1,0:T(8,128)}, /*index=5*/f32[768,768]{1,0:T(8,128)}) custom-call(bf16[2,2,2,4,24,1152]{5,4,3,2,1,0:T(8,128)(2,1)S(1)} %copy-done.2, bf16[2,2,2,4,24,1152]{5,4,3,2,1,0:T(8,128)(2,1)S(1)} %copy-done.3, ...), custom_call_target="tpu_custom_call" | custom-call | tf_op jit(solution)/shard_map/pallas_call | solution.py:741
  149.8 0.1 reshape.244
  149.9 0.1 reshape.245
  150.0 0.7 dynamic_slice.18
  150.6 1.5 fusion.36
  152.2 1.3 slice_reduce_fusion.4
  153.5 0.6 copy.55
  (67 shorter events, 0.6 us)
Async XLA Ops:
  0.7 49.4 %copy-start = (bf16[768,768]{1,0:T(8,128)(2,1)S(1)}, bf16[768,768]{1,0:T(8,128)(2,1)}, u32[]{:S(2)}) copy-start(bf16[768,768]{1,0:T(8,128)(2,1)} %param.21) | copy-start | bytes 3538948
  0.7 2.7 %copy-start.16 = (bf16[576]{0:T(1024)(128)(2,1)S(1)}, bf16[576]{0:T(1024)(128)(2,1)}, u32[]{:S(2)}) copy-start(bf16[576]{0:T(1024)(128)(2,1)} %param.16) | copy-start | bytes 3460
  0.7 2.8 %copy-start.17 = (bf16[192]{0:T(256)(128)(2,1)S(1)}, bf16[192]{0:T(256)(128)(2,1)}, u32[]{:S(2)}) copy-start(bf16[192]{0:T(256)(128)(2,1)} %param.18) | copy-start | bytes 1156
  0.7 2.8 %copy-start.18 = (bf16[192]{0:T(256)(128)(2,1)S(1)}, bf16[192]{0:T(256)(128)(2,1)}, u32[]{:S(2)}) copy-start(bf16[192]{0:T(256)(128)(2,1)} %param.22) | copy-start | bytes 1156
  0.7 2.8 %copy-start.19 = (bf16[192]{0:T(256)(128)(2,1)S(1)}, bf16[192]{0:T(256)(128)(2,1)}, u32[]{:S(2)}) copy-start(bf16[192]{0:T(256)(128)(2,1)} %param.23) | copy-start | bytes 1156
  0.7 2.8 %copy-start.20 = (bf16[192]{0:T(256)(128)(2,1)S(1)}, bf16[192]{0:T(256)(128)(2,1)}, u32[]{:S(2)}) copy-start(bf16[192]{0:T(256)(128)(2,1)} %param.24) | copy-start | bytes 1156
  0.7 2.8 %copy-start.21 = (bf16[192]{0:T(256)(128)(2,1)S(1)}, bf16[192]{0:T(256)(128)(2,1)}, u32[]{:S(2)}) copy-start(bf16[192]{0:T(256)(128)(2,1)} %param.25) | copy-start | bytes 1156
  0.7 2.8 %copy-start.22 = (bf16[192]{0:T(256)(128)(2,1)S(1)}, bf16[192]{0:T(256)(128)(2,1)}, u32[]{:S(2)}) copy-start(bf16[192]{0:T(256)(128)(2,1)} %param.26) | copy-start | bytes 1156
  0.7 2.9 %copy-start.8 = (bf16[128,768]{1,0:T(8,128)(2,1)S(1)}, bf16[128,768]{1,0:T(8,128)(2,1)}, u32[]{:S(2)}) copy-start(bf16[128,768]{1,0:T(8,128)(2,1)} %x_ref.3) | copy-start | bytes 589828
  0.7 2.9 %copy-start.4 = (bf16[128,768]{1,0:T(8,128)(2,1)S(1)}, bf16[128,768]{1,0:T(8,128)(2,1)}, u32[]{:S(2)}) copy-start(bf16[128,768]{1,0:T(8,128)(2,1)} %c_ref.3) | copy-start | bytes 589828
  37.1 0.9 copy-start.6
  38.6 2.0 %copy-start.7 = (bf16[2,2,2,4,24,576]{5,4,3,2,1,0:T(8,128)(2,1)S(1)}, bf16[2,2,2,4,24,576]{5,4,3,2,1,0:T(8,128)(2,1)}, u32[]{:S(2)}) copy-start(bf16[2,2,2,4,24,576]{5,4,3,2,1,0:T(8,128)(2,1)} %copy-done.6) | copy-start | bytes 2654212
  45.1 1.0 copy-start.10
  47.5 1.3 copy-start.9
  48.0 0.9 copy-start.15
  48.0 1.2 copy-start.12
  56.1 1.2 copy-start.11
  70.2 70.8 %copy-start.1 = (bf16[4,256,768]{2,1,0:T(8,128)(2,1)S(1)}, bf16[4,256,768]{2,1,0:T(8,128)(2,1)}, u32[]{:S(2)}) copy-start(bf16[4,256,768]{2,1,0:T(8,128)(2,1)} %pad_maximum_fusion.parts_ref) | copy-start | bytes 4718596
  141.0 1.5 copy-start.2
  142.5 1.5 copy-start.3
  143.9 1.3 copy-start.5
  145.2 4.6 %copy-start.13 = (f32[4,576]{1,0:T(4,128)S(1)}, f32[4,576]{1,0:T(4,128)}, u32[]{:S(2)}) copy-start(f32[4,576]{1,0:T(4,128)} %get-tuple-element.41) | copy-start | bytes 27652
  152.2 1.9 %copy-start.14 = (f32[1,192]{1,0:T(1,128)}, f32[1,192]{1,0:T(1,128)S(1)}, u32[]{:S(2)}) copy-start(f32[1,192]{1,0:T(1,128)S(1)} %get-tuple-element.82) | copy-start | bytes 2308
